TPU v7x, 128 devices: a whole 4x4x4 slice. The times are simulated.
128 devices in a mesh: panel: 32 (over y, z_lo, x), span: 4 (over z_hi, core).
Axes of the slice: x: 4, y: 4, z: 4 (z_hi: 2, z_lo: 2; z = z_hi * 2 + z_lo), core: 2. Of those that a mesh axis runs over, the one named last changes fastest.
Arguments:
- state: float32 [4, 44, 4096, 512], P('span', None, 'panel'), may hold values from -6 to 6
- wind_field: float32 [2, 4096, 512], P(None, 'panel'), may hold values from -0.45 to 0.45
- level_scale: float32 [44], replicated, may hold values from 0.3 to 1
- edge_flip: int32 [32], replicated, may hold values 0 or 1
- block_dest: int32 [32, 32], replicated, may hold values from 0 to 31, as said below
- weight_in: bfloat16 [176, 512], replicated, may hold values from -0.4375 to 0.4375
- weight_mid: bfloat16 [4, 512, 512], replicated, may hold values from -0.25 to 0.25
- weight_out: bfloat16 [512, 176], replicated, may hold values from -0.25 to 0.25
Outputs:
- new_state: float32 [4, 44, 4096, 512], P('span', None, 'panel')
- heating: float32 [524288], P(('panel', 'span'))
Inputs may be any that keep to these rules, and one draw needn't show every extreme that they name: Each row of block_dest is a permutation of 0 to 31.
All inputs are finite; a program needn't handle non-finite values.
Results may differ from a plain program's by a relative error of at most 0.014.
Values may be sent and summed in bfloat16 or wider, within the bound.
No kernel may reach another device: no remote copies, remote signals or barrier semaphores. Data moves between devices by JAX's collectives and lax.ppermute only.
A program may use at most 192 MiB of HBM per device.

v0:
```python
import jax
import jax.numpy as jnp
from jax import lax
from jax.experimental import pallas as pl
from jax.experimental.pallas import tpu as pltpu
from jax.sharding import PartitionSpec as P


F = 4
L = 44
LP = 48
BY = 128
NX = 512
HID = 512
NB = 32
K = 2
ORDER = (0, 1)
R = BY // K
NBK = R // 4
SB = 8
CH = 4
G = 16
ROOM = 59 << 20
LV = 11
NG = L // LV
AXES = ("panel", "span")
f32 = jnp.float32
bf16 = jnp.bfloat16


def lane_iota(shape):
    return lax.broadcasted_iota(jnp.int32, shape, len(shape) - 1)


def row_iota(shape):
    return lax.broadcasted_iota(jnp.int32, shape, len(shape) - 2)


def shift_right(tiles):
    n = len(tiles)
    rolled = [pltpu.roll(t, 1, 1) for t in tiles]
    first = lane_iota(tiles[0].shape) == 0
    return [jnp.where(first, rolled[(t - 1) % n], rolled[t]) for t in range(n)]


def shift_left(tiles):
    n = len(tiles)
    rolled = [pltpu.roll(t, 127, 1) for t in tiles]
    last = lane_iota(tiles[0].shape) == 127
    return [jnp.where(last, rolled[(t + 1) % n], rolled[t]) for t in range(n)]


def advect_body(k, *refs):
    top = k == 0
    bottom = k == K - 1
    refs = list(refs)
    scal = refs.pop(0)
    scale = refs.pop(0)
    state = refs.pop(0)
    wind = refs.pop(0)
    halo = refs.pop(0) if top or bottom else None
    moved = refs.pop(0)
    msgs = [refs.pop(0) for _ in range(4)]
    cells, out, coef, pool, in_sem, out_sem = refs[:6]
    edge = refs[6] if top or bottom else None
    off = 0 if top else 8
    r0 = k * R
    first = r0 - off
    count = R + 16 - (8 if top else 0) - (8 if bottom else 0)

    def fetch(g, t):
        return pltpu.make_async_copy(
            state.at[pl.ds(g * LV, LV), first : first + count, 128 * t : 128 * (t + 1)],
            cells.at[t, pl.ds(g * LV, LV)],
            in_sem.at[g, t],
        )

    def store(g):
        return pltpu.make_async_copy(
            out.at[pl.ds(g * LV, LV)], moved.at[pl.ds(g * LV, LV)], out_sem.at[g]
        )

    for g in range(NG):
        for t in range(4):
            fetch(g, t).start()
    if edge is not None:
        flag = scal[1] if top else scal[2]
        anti = (row_iota((128, 128)) + lane_iota((128, 128)) == 127).astype(f32)
        for t in range(4):
            turned = jnp.dot(
                halo[:, 128 * (3 - t) : 128 * (4 - t)],
                anti,
                precision=lax.Precision.HIGHEST,
                preferred_element_type=f32,
            )
            edge[t, 0 : L + 1] = jnp.where(flag == 1, turned, halo[:, 128 * t : 128 * (t + 1)])
    cols = [slice(128 * t, 128 * (t + 1)) for t in range(4)]
    u = [wind[0, r0 : r0 + R, c] for c in cols]
    v = [wind[1, r0 : r0 + R, c] for c in cols]
    rows = row_iota((R, 128))
    if top:
        above = [
            jnp.where(rows == 0, edge[t, L : L + 1], pltpu.roll(w, 1, 0)) for t, w in enumerate(v)
        ]
    else:
        above = [wind[1, r0 - 1 : r0 + R - 1, c] for c in cols]
    if bottom:
        below = [
            jnp.where(rows == R - 1, edge[t, L : L + 1], pltpu.roll(w, R - 1, 0))
            for t, w in enumerate(v)
        ]
    else:
        below = [wind[1, r0 + 1 : r0 + R + 1, c] for c in cols]
    left = shift_right(u)
    face = [0.5 * (a + b) for a, b in zip(left, u)]
    plus = [jnp.maximum(w, 0.0) for w in face]
    minus = [jnp.minimum(w, 0.0) for w in face]
    next_plus = shift_left(plus)
    next_minus = shift_left(minus)
    for t in range(4):
        lower = 0.5 * (above[t] + v[t])
        upper = 0.5 * (v[t] + below[t])
        lower_plus = jnp.maximum(lower, 0.0)
        lower_minus = jnp.minimum(lower, 0.0)
        upper_plus = jnp.maximum(upper, 0.0)
        upper_minus = jnp.minimum(upper, 0.0)
        coef[5 * t] = next_plus[t] - minus[t] + upper_plus - lower_minus
        coef[5 * t + 1] = next_minus[t]
        coef[5 * t + 2] = -plus[t]
        coef[5 * t + 3] = upper_minus
        coef[5 * t + 4] = -lower_plus
    quarter = jnp.where(row_iota((256, 128)) // 2 == lane_iota((256, 128)), 0.25, 0.0).astype(bf16)

    def level(l, carry):
        s = scale[l]
        rows = row_iota((G, 128))
        for n in range(R // G):
            at = off + n * G
            q = [cells[t, l, at : at + G, :] for t in range(4)]
            left = shift_right(q)
            right = shift_left(q)
            for t in range(4):
                if top and n == 0:
                    up = jnp.where(rows == 0, edge[t, pl.ds(l, 1), :], pltpu.roll(q[t], 1, 0))
                else:
                    up = cells[t, l, at - 1 : at + G - 1, :]
                if bottom and n == R // G - 1:
                    down = jnp.where(rows == G - 1, edge[t, pl.ds(l, 1), :], pltpu.roll(q[t], G - 1, 0))
                else:
                    down = cells[t, l, at + 1 : at + G + 1, :]
                band = slice(n * G, (n + 1) * G)
                change = (
                    coef[5 * t, band] * q[t]
                    + coef[5 * t + 1, band] * right[t]
                    + coef[5 * t + 2, band] * left[t]
                    + coef[5 * t + 3, band] * down
                    + coef[5 * t + 4, band] * up
                )
                out[l, band, 128 * t : 128 * (t + 1)] = q[t] - s * change
        return carry

    def group(g, carry):
        for t in range(4):
            fetch(g, t).wait()
        lax.fori_loop(g * LV, (g + 1) * LV, level, 0)
        store(g).start()
        for half in range(2):
            block = out[pl.ds(g * LV, LV), :, 256 * half : 256 * (half + 1)].reshape(LV * R, 256)
            high = block.astype(bf16)
            low = (block - high.astype(f32)).astype(bf16)
            pooled = jnp.dot(high, quarter, preferred_element_type=f32)
            pooled += jnp.dot(low, quarter, preferred_element_type=f32)
            pooled += pltpu.roll(pooled, LV * R - 1, 0)
            start = pl.multiple_of(half * LP * R + g * (LV * R), 8)
            pool[pl.ds(start, LV * R), :] = pooled
        return carry

    lax.fori_loop(0, NG, group, 0)
    valid = row_iota((LP, 128)) < L
    for i in range(4):
        c = scal[0] ^ i
        base = (c & 1) * (LP * R) + (c >> 1) * 2
        for b in range(NBK):
            pair = pool[pl.ds(base + 4 * b, LP, stride=R), :]
            msgs[i][b] = jnp.where(valid, pair, 0.0).astype(bf16)
    for g in range(NG):
        store(g).wait()


def advect_call(k, scal, scale, state, wind, halo):
    top = k == 0
    bottom = k == K - 1
    count = R + 16 - (8 if top else 0) - (8 if bottom else 0)
    smem = pl.BlockSpec(memory_space=pltpu.SMEM)
    vmem = pl.BlockSpec(memory_space=pltpu.VMEM)
    hbm = pl.BlockSpec(memory_space=pltpu.HBM)
    in_specs = [smem, smem, hbm, vmem]
    operands = [scal, scale, state, wind]
    scratch = [
        pltpu.VMEM((4, L, count, 128), f32),
        pltpu.VMEM((L, R, NX), f32),
        pltpu.VMEM((20, R, 128), f32),
        pltpu.VMEM((2 * LP * R, 128), f32),
        pltpu.SemaphoreType.DMA((NG, 4)),
        pltpu.SemaphoreType.DMA((NG,)),
    ]
    if top or bottom:
        in_specs.append(vmem)
        operands.append(halo)
        scratch.append(pltpu.VMEM((4, LP, 128), f32))
    out_shape = [jax.ShapeDtypeStruct((L, R, NX), f32)]
    out_shape += [jax.ShapeDtypeStruct((NBK, LP, 128), bf16)] * 4

    def body(*refs):
        advect_body(k, *refs)

    return pl.pallas_call(
        body,
        out_shape=out_shape,
        in_specs=in_specs,
        out_specs=[hbm] + [vmem] * 4,
        compiler_params=pltpu.CompilerParams(vmem_limit_bytes=ROOM),
        scratch_shapes=scratch,
    )(*operands)


def silu(z):
    half = 0.5 * z
    return half + half * jnp.tanh(half)


def network_body(scal, dest, m0, m1, m2, m3, w_in, w_mid, w_out, heat_in, o0, o1, o2, o3, heat, xs, ts):
    c = scal[0]
    heat[...] = heat_in[...]
    ins = (m0, m1, m2, m3)
    outs = (o0, o1, o2, o3)
    for i in range(4):
        at = pl.multiple_of((c ^ i) * LP, LP)
        for b in range(NBK):
            xs[b // SB, pl.ds(at, LP), 128 * (b % SB) : 128 * (b % SB + 1)] = ins[i][b]

    def part(j, carry):
        wide = xs[j].astype(f32)
        inv = lax.rsqrt(jnp.sum(wide * wide, axis=0, keepdims=True) * (1.0 / (F * L)) + 1e-05)
        normed = (wide * inv).T.astype(bf16)
        size = SB * 128 // CH
        hid = []
        for n in range(CH):
            z = jnp.dot(normed[n * size : (n + 1) * size], w_in[...], preferred_element_type=f32)
            hid.append(silu(z).astype(bf16))
        for layer in range(4):
            for n in range(CH):
                z = jnp.dot(hid[n], w_mid[layer], preferred_element_type=f32)
                hid[n] = (hid[n].astype(f32) + silu(z)).astype(bf16)
        parts = [jnp.dot(h, w_out[...], preferred_element_type=f32).T for h in hid]
        for n in range(CH):
            ts[j, :, n * size : (n + 1) * size] = parts[n].astype(bf16)
            warm = jnp.sum(parts[n][0:L], axis=0, keepdims=True) * (L**-0.5)
            for b in range(SB // CH):
                heat[pl.ds(dest[j * SB + n * (SB // CH) + b], 1), :] = warm[:, 128 * b : 128 * (b + 1)]
        return carry

    lax.fori_loop(0, NBK // SB, part, 0)
    for i in range(4):
        at = pl.multiple_of((c ^ i) * LP, LP)
        for b in range(NBK):
            outs[i][b] = ts[b // SB, pl.ds(at, LP), 128 * (b % SB) : 128 * (b % SB + 1)]


def network_call(scal, dest, msgs, w_in, w_mid, w_out, heat):
    smem = pl.BlockSpec(memory_space=pltpu.SMEM)
    vmem = pl.BlockSpec(memory_space=pltpu.VMEM)
    shape = jax.ShapeDtypeStruct((NBK, LP, 128), bf16)
    return pl.pallas_call(
        network_body,
        out_shape=[shape] * 4 + [jax.ShapeDtypeStruct((NB, 128), f32)],
        in_specs=[smem, smem] + [vmem] * 8,
        out_specs=[vmem] * 5,
        compiler_params=pltpu.CompilerParams(vmem_limit_bytes=ROOM),
        scratch_shapes=[
            pltpu.VMEM((NBK // SB, F * LP, SB * 128), bf16),
            pltpu.VMEM((NBK // SB, F * LP, SB * 128), bf16),
        ],
    )(scal, dest, *msgs, w_in, w_mid, w_out, heat)


def apply_body(k, first, *refs):
    refs = list(refs)
    scal = refs.pop(0)
    ins = [refs.pop(0) for _ in range(4)]
    moved = refs.pop(0)
    if not first:
        refs.pop(0)
    final, cells, spread, in_sem, out_sem = refs

    def fetch(g):
        return pltpu.make_async_copy(
            moved.at[pl.ds(g * LV, LV)], cells.at[pl.ds(g * LV, LV)], in_sem.at[g]
        )

    def store(g):
        return pltpu.make_async_copy(
            cells.at[pl.ds(g * LV, LV)],
            final.at[0, pl.ds(g * LV, LV), k * R : (k + 1) * R, :],
            out_sem.at[g],
        )

    for g in range(NG):
        fetch(g).start()
    for i in range(4):
        c = scal[0] ^ i
        base = (c & 1) * (LP * R) + (c >> 1) * 2
        for b in range(NBK):
            spread[pl.ds(base + 4 * b, LP, stride=R), :] = ins[i][b].astype(f32)
    twice = (row_iota((128, 256)) == lane_iota((128, 256)) // 2).astype(bf16)
    even = row_iota((LV * R, 128)) % 2 == 0

    def group(g, carry):
        fetch(g).wait()
        for half in range(2):
            start = pl.multiple_of(half * LP * R + g * (LV * R), 8)
            coarse = spread[pl.ds(start, LV * R), :]
            coarse = jnp.where(even, coarse, pltpu.roll(coarse, 1, 0)).astype(bf16)
            fine = jnp.dot(coarse, twice, preferred_element_type=f32)
            lanes = slice(256 * half, 256 * (half + 1))
            at = pl.ds(g * LV, LV)
            cells[at, :, lanes] = cells[at, :, lanes] + fine.reshape(LV, R, 256)
        store(g).start()
        return carry

    lax.fori_loop(0, NG, group, 0)
    for g in range(NG):
        store(g).wait()


def apply_call(k, scal, tends, moved, buffer):
    smem = pl.BlockSpec(memory_space=pltpu.SMEM)
    vmem = pl.BlockSpec(memory_space=pltpu.VMEM)
    hbm = pl.BlockSpec(memory_space=pltpu.HBM)
    in_specs = [smem] + [vmem] * 4 + [hbm]
    operands = [scal, *tends, moved]
    aliases = {}
    if buffer is not None:
        in_specs.append(hbm)
        operands.append(buffer)
        aliases = {6: 0}

    def body(*refs):
        apply_body(k, buffer is None, *refs)

    return pl.pallas_call(
        body,
        out_shape=jax.ShapeDtypeStruct((1, L, BY, NX), f32),
        in_specs=in_specs,
        out_specs=hbm,
        scratch_shapes=[
            pltpu.VMEM((L, R, NX), f32),
            pltpu.VMEM((2 * LP * R, 128), f32),
            pltpu.SemaphoreType.DMA((NG,)),
            pltpu.SemaphoreType.DMA((NG,)),
        ],
        compiler_params=pltpu.CompilerParams(vmem_limit_bytes=ROOM),
        input_output_aliases=aliases,
    )(*operands)


def ring(step):
    return [(i, (i + step) % NB) for i in range(NB)]


def cross(i):
    return [(p * F + s, (p ^ 4) * F + (s ^ i)) for p in range(NB) for s in range(F)]


def local(state, wind, level_scale, edge_flip, block_dest, weight_in, weight_mid, weight_out):
    here = lax.axis_index("panel")
    span = lax.axis_index("span")
    first = jnp.concatenate([state[0, :, 0, :], wind[1, 0:1, :]], axis=0)
    last = jnp.concatenate([state[0, :, BY - 1, :], wind[1, BY - 1 :, :]], axis=0)
    above = lax.ppermute(last, "panel", ring(1))
    below = lax.ppermute(first, "panel", ring(-1))
    scal = jnp.stack([span, edge_flip[here], edge_flip[(here + 1) % NB]]).astype(jnp.int32)
    served = lax.dynamic_slice_in_dim(block_dest, here ^ 4, 1, 0)[0]
    w_in = jnp.pad(weight_in.reshape(F, L, HID), ((0, 0), (0, LP - L), (0, 0))).reshape(F * LP, HID)
    w_out = jnp.pad(weight_out.reshape(HID, F, L), ((0, 0), (0, 0), (0, LP - L))).reshape(HID, F * LP)
    field = state[0]
    moved = {}
    arrived = {}
    for k in ORDER:
        halo = above if k == 0 else below
        moved[k], *msgs = advect_call(k, scal, level_scale, field, wind, halo)
        arrived[k] = [lax.ppermute(m, AXES, cross(i)) for i, m in enumerate(msgs)]
    heat = jnp.zeros((NB, 128), f32)
    returned = {}
    for k in ORDER:
        dest = lax.slice_in_dim(served, k * NBK, (k + 1) * NBK)
        *tends, heat = network_call(scal, dest, arrived[k], w_in, weight_mid, w_out, heat)
        returned[k] = [lax.ppermute(t, AXES, cross(i)) for i, t in enumerate(tends)]
    slots = lax.all_to_all(heat, "panel", split_axis=0, concat_axis=0, tiled=True)
    heating = slots.reshape(4, 2, 4, 128)[:, ::-1].reshape(NB * 128)
    new_state = None
    for k in ORDER:
        new_state = apply_call(k, scal, returned[k], moved[k], new_state)
    return (new_state, heating)


def solution(mesh):
    placed = (P("span", None, "panel", None), P(None, "panel", None), P(), P(), P(), P(), P(), P())
    return jax.shard_map(
        local,
        mesh=mesh,
        in_specs=placed,
        out_specs=(P("span", None, "panel", None), P(("panel", "span"))),
        check_vma=False,
    )
```

profile of v0, /device:TPU:1, one launch (start us, length us, event | category | flops | bytes accessed | tf_op | source)
XLA Modules:
  0.0 113.5 jit_solution(1755794962685380298)
XLA Ops:
  0.6 0.0 copy-start
  0.7 0.8 slice_bitcast_fusion
  1.5 1.5 %fusion = (f32[1,44,1,512]{3,2,1,0:T(1,128)S(1)}, f32[1,44,1,512]{3,2,1,0:T(1,128)S(1)}) fusion(f32[1,44,128,512]{3,2,1,0:T(8,128)} %param.8), kind=kLoop, calls=%fused_computation.10 | loop fusion | bytes 360448 | tf_op jit(solution)/shard_map/slice | solution.py:379
  3.0 2.1 %collective-permute-start.5 = (f32[45,512]{1,0:T(8,128)S(1)}, f32[45,512]{1,0:T(8,128)S(1)}, u32[]{:S(2)}, u32[]{:S(2)}) collective-permute-start(f32[45,512]{1,0:T(8,128)S(1)} %pad_maximum_fusion.1), channel_id=1, source_target_pairs={{0,4},{4,8},{8,12},{12,16},{16,20},{20,24},{24,28},{28,32},{32,36}... | collective-permute-start | bytes 276488 | tf_op jit(solution)/shard_map/ppermute | solution.py:380
  5.1 1.3 %fusion.1 = (s32[1]{0:T(128)}, s32[1]{0:T(128)}) fusion(s32[32]{0:T(128)} %param.11, s32[]{:T(128)S(6)} %select_n.16, s32[]{:T(128)S(6)} %select_n.18), kind=kLoop, calls=%fused_computation.11 | loop fusion | bytes 24 | tf_op jit(solution)/shard_map/dynamic_slice | solution.py:382
  6.4 1.9 %pad_add_fusion.refs_0_.scal = s32[3]{0:T(128)} fusion(s32[1]{0:T(128)} %get-tuple-element.49, s32[1]{0:T(128)} %get-tuple-element.48, s32[1]{0:T(128)} %bitcast), kind=kLoop, calls=%fused_computation.6 | loop fusion | flops 6 | bytes 24 | tf_op jit(solution)/shard_map/stack | solution.py:382
  8.4 4.3 %collective-permute-done.5.refs_4_ = f32[45,512]{1,0:T(8,128)S(1)} collective-permute-done((f32[45,512]{1,0:T(8,128)S(1)}, f32[45,512]{1,0:T(8,128)S(1)}, u32[]{:S(2)}, u32[]{:S(2)}) %collective-permute-start.5) | collective-permute-done | bytes 92192 | tf_op jit(solution)/shard_map/ppermute | solution.py:380
  12.7 0.6 copy-done.19
  13.3 13.7 %shard_map.96 = (f32[44,64,512]{2,1,0:T(8,128)}, bf16[16,48,128]{2,1,0:T(8,128)(2,1)}, bf16[16,48,128]{2,1,0:T(8,128)(2,1)}, bf16[16,48,128]{2,1,0:T(8,128)(2,1)}, bf16[16,48,128]{2,1,0:T(8,128)(2,1)}) custom-call(s32[3]{0:T(128)} %pad_add_fusion.refs_0_.scal, f32[44]{0:T(128)} %refs_1_.3, f32[44,128,512]{2,1,0:T(8,128)} %bitcast.25, ...), custom_call_target="tpu_custom_call" | custom-call | tf_op jit(solution)/shard_map/pallas_call | solution.py:217
  27.0 0.1 collective-permute-start.6
  27.1 2.2 %collective-permute-start = (f32[45,512]{1,0:T(8,128)S(1)}, f32[45,512]{1,0:T(8,128)S(1)}, u32[]{:S(2)}, u32[]{:S(2)}) collective-permute-start(f32[45,512]{1,0:T(8,128)S(1)} %pad_maximum_fusion), channel_id=1, source_target_pairs={{0,124},{4,0},{8,4},{12,8},{16,12},{20,16},{24,20},{28,24},{32,28}... | collective-permute-start | bytes 276488 | tf_op jit(solution)/shard_map/ppermute | solution.py:381
  29.4 0.0 copy-done.18
  29.4 0.7 pad.8
  30.1 0.8 copy.21.w_out
  31.0 0.8 collective-permute-start.7
  31.8 4.2 %collective-permute-start.8 = (bf16[16,48,128]{2,1,0:T(8,128)(2,1)}, bf16[16,48,128]{2,1,0:T(8,128)(2,1)S(1)}, u32[]{:S(2)}, u32[]{:S(2)}) collective-permute-start(bf16[16,48,128]{2,1,0:T(8,128)(2,1)} %get-tuple-element.28), channel_id=1, source_target_pairs={{0,18},{1,19},{2,16},{3,17},{4,22},{5,23},{6,20},{7,21},{8,26},{9,... | collective-permute-start | bytes 589832 | tf_op jit(solution)/shard_map/ppermute | solution.py:392
  36.0 0.0 collective-permute-start.9
  36.0 0.0 collective-permute-done.refs_4_
  36.1 0.6 copy-done.20
  36.7 13.8 %shard_map.95 = (f32[44,64,512]{2,1,0:T(8,128)}, bf16[16,48,128]{2,1,0:T(8,128)(2,1)}, bf16[16,48,128]{2,1,0:T(8,128)(2,1)}, bf16[16,48,128]{2,1,0:T(8,128)(2,1)}, bf16[16,48,128]{2,1,0:T(8,128)(2,1)}) custom-call(s32[3]{0:T(128)} %pad_add_fusion.refs_0_.scal, f32[44]{0:T(128)} %refs_1_.3, f32[44,128,512]{2,1,0:T(8,128)} %bitcast.26, ...), custom_call_target="tpu_custom_call" | custom-call | tf_op jit(solution)/shard_map/pallas_call | solution.py:217
  50.4 0.1 collective-permute-start.1
  50.5 0.0 collective-permute-done.6.m0
  50.6 2.0 %collective-permute-start.2 = (bf16[16,48,128]{2,1,0:T(8,128)(2,1)}, bf16[16,48,128]{2,1,0:T(8,128)(2,1)S(1)}, u32[]{:S(2)}, u32[]{:S(2)}) collective-permute-start(bf16[16,48,128]{2,1,0:T(8,128)(2,1)} %get-tuple-element.23), channel_id=1, source_target_pairs={{0,17},{1,16},{2,19},{3,18},{4,21},{5,20},{6,23},{7,22},{8,25},{9,... | collective-permute-start | bytes 589832 | tf_op jit(solution)/shard_map/ppermute | solution.py:392
  52.6 0.7 slice_bitcast_fusion.2
  53.2 0.0 collective-permute-done.7.m1
  53.2 2.7 %collective-permute-start.3 = (bf16[16,48,128]{2,1,0:T(8,128)(2,1)}, bf16[16,48,128]{2,1,0:T(8,128)(2,1)S(1)}, u32[]{:S(2)}, u32[]{:S(2)}) collective-permute-start(bf16[16,48,128]{2,1,0:T(8,128)(2,1)} %get-tuple-element.24), channel_id=1, source_target_pairs={{0,18},{1,19},{2,16},{3,17},{4,22},{5,23},{6,20},{7,21},{8,26},{9,... | collective-permute-start | bytes 589832 | tf_op jit(solution)/shard_map/ppermute | solution.py:392
  55.9 0.0 collective-permute-done.8.m2
  55.9 0.0 collective-permute-start.4
  55.9 0.0 collective-permute-done.9.m3
  55.9 0.7 broadcast_in_dim.3.heat_in
  56.6 0.0 copy-done.16
  56.7 10.7 %shard_map.97 = (bf16[16,48,128]{2,1,0:T(8,128)(2,1)}, bf16[16,48,128]{2,1,0:T(8,128)(2,1)}, bf16[16,48,128]{2,1,0:T(8,128)(2,1)}, bf16[16,48,128]{2,1,0:T(8,128)(2,1)}, f32[32,128]{1,0:T(8,128)}) custom-call(s32[3]{0:T(128)} %pad_add_fusion.refs_0_.scal, s32[16]{0:T(128)} %get-tuple-element.46.dest, bf16[16,48,128]{2,1,0:T(8,128)(2,1)} %copy-done.9, ...), custom_call_target="tpu_custom_call" | custom-call | tf_op jit(solution)/shard_map/pallas_call | solution.py:274
  67.3 0.0 collective-permute-start.14
  67.3 0.0 collective-permute-done.1.m0
  67.4 2.1 %collective-permute-start.15 = (bf16[16,48,128]{2,1,0:T(8,128)(2,1)}, bf16[16,48,128]{2,1,0:T(8,128)(2,1)S(1)}, u32[]{:S(2)}, u32[]{:S(2)}) collective-permute-start(bf16[16,48,128]{2,1,0:T(8,128)(2,1)} %get-tuple-element.37), channel_id=1, source_target_pairs={{0,17},{1,16},{2,19},{3,18},{4,21},{5,20},{6,23},{7,22},{8,25},{9,... | collective-permute-start | bytes 589832 | tf_op jit(solution)/shard_map/ppermute | solution.py:398
  69.4 0.0 collective-permute-done.2.m1
  69.4 2.6 %collective-permute-start.16 = (bf16[16,48,128]{2,1,0:T(8,128)(2,1)}, bf16[16,48,128]{2,1,0:T(8,128)(2,1)S(1)}, u32[]{:S(2)}, u32[]{:S(2)}) collective-permute-start(bf16[16,48,128]{2,1,0:T(8,128)(2,1)} %get-tuple-element.38), channel_id=1, source_target_pairs={{0,18},{1,19},{2,16},{3,17},{4,22},{5,23},{6,20},{7,21},{8,26},{9,... | collective-permute-start | bytes 589832 | tf_op jit(solution)/shard_map/ppermute | solution.py:398
  72.0 0.0 collective-permute-done.3.m2
  72.0 0.0 collective-permute-start.17
  72.1 0.0 collective-permute-done.4.m3
  72.1 0.6 copy-done.12
  72.7 0.1 copy-done.14
  72.7 10.7 %shard_map.98 = (bf16[16,48,128]{2,1,0:T(8,128)(2,1)}, bf16[16,48,128]{2,1,0:T(8,128)(2,1)}, bf16[16,48,128]{2,1,0:T(8,128)(2,1)}, bf16[16,48,128]{2,1,0:T(8,128)(2,1)}, f32[32,128]{1,0:T(8,128)}) custom-call(s32[3]{0:T(128)} %pad_add_fusion.refs_0_.scal, s32[16]{0:T(128)} %get-tuple-element.47.dest, bf16[16,48,128]{2,1,0:T(8,128)(2,1)} %copy-done.10, ...), custom_call_target="tpu_custom_call" | custom-call | tf_op jit(solution)/shard_map/pallas_call | solution.py:274
  83.4 0.0 collective-permute-start.10
  83.4 0.0 collective-permute-done.14.refs_1_
  83.5 2.1 %collective-permute-start.11 = (bf16[16,48,128]{2,1,0:T(8,128)(2,1)}, bf16[16,48,128]{2,1,0:T(8,128)(2,1)S(1)}, u32[]{:S(2)}, u32[]{:S(2)}) collective-permute-start(bf16[16,48,128]{2,1,0:T(8,128)(2,1)} %get-tuple-element.32), channel_id=1, source_target_pairs={{0,17},{1,16},{2,19},{3,18},{4,21},{5,20},{6,23},{7,22},{8,25},{9,... | collective-permute-start | bytes 589832 | tf_op jit(solution)/shard_map/ppermute | solution.py:398
  85.5 0.0 collective-permute-done.15.refs_2_
  85.5 2.6 %collective-permute-start.12 = (bf16[16,48,128]{2,1,0:T(8,128)(2,1)}, bf16[16,48,128]{2,1,0:T(8,128)(2,1)S(1)}, u32[]{:S(2)}, u32[]{:S(2)}) collective-permute-start(bf16[16,48,128]{2,1,0:T(8,128)(2,1)} %get-tuple-element.33), channel_id=1, source_target_pairs={{0,18},{1,19},{2,16},{3,17},{4,22},{5,23},{6,20},{7,21},{8,26},{9,... | collective-permute-start | bytes 589832 | tf_op jit(solution)/shard_map/ppermute | solution.py:398
  88.1 0.0 collective-permute-done.16.refs_3_
  88.1 0.0 collective-permute-start.13
  88.2 11.5 %all_to_all.9 = f32[32,1,128]{2,1,0:T(1,128)S(1)} all-to-all(f32[32,1,128]{2,1,0:T(1,128)} %bitcast.34), channel_id=1, replica_groups=mesh['panel'=32,'span'=4] {'panel'}, dimensions={0} | all-to-all | bytes 32768 | tf_op jit(solution)/shard_map/all_to_all | solution.py:399
  99.7 0.6 rev.3
  100.3 0.0 collective-permute-done.17.refs_4_
  100.3 0.7 copy-done.4
  101.0 5.7 %shard_map.99.refs_6_ = f32[1,44,128,512]{3,2,1,0:T(8,128)} custom-call(s32[3]{0:T(128)} %pad_add_fusion.refs_0_.scal, bf16[16,48,128]{2,1,0:T(8,128)(2,1)} %copy-done.1, bf16[16,48,128]{2,1,0:T(8,128)(2,1)} %copy-done.2, bf16[16,48,128]{2,1,0:T(8,128)(2,1)} %copy-done.3, bf16[16,48,128]{2,1,0:T(8,128)(2,1)} %copy-done.4, ...), custom_call_target="tpu_custom_call" | custom-call | tf_op jit(solution)/shard_map/pallas_call | solution.py:351
  106.7 0.0 collective-permute-done.10.refs_1_
  106.7 0.0 collective-permute-done.11.refs_2_
  106.8 0.0 collective-permute-done.12.refs_3_
  106.8 0.0 collective-permute-done.13.refs_4_
  106.8 0.6 copy-done.5
  107.4 0.1 copy-done.6
  107.5 0.1 copy-done.7
  107.6 0.0 copy-done.8
  107.6 5.7 %shard_map.100 = f32[1,44,128,512]{3,2,1,0:T(8,128)} custom-call(s32[3]{0:T(128)} %pad_add_fusion.refs_0_.scal, bf16[16,48,128]{2,1,0:T(8,128)(2,1)} %copy-done.5, bf16[16,48,128]{2,1,0:T(8,128)(2,1)} %copy-done.6, bf16[16,48,128]{2,1,0:T(8,128)(2,1)} %copy-done.7, bf16[16,48,128]{2,1,0:T(8,128)(2,1)} %copy-done.8, ...), custom_call_target="tpu_custom_call", output_to_operand_aliasing={{}: (6, {})} | custom-call | tf_op jit(solution)/shard_map/pallas_call | solution.py:351
  (38 shorter events, 0.2 us)
Async XLA Ops:
  0.6 30.3 %copy-start = (s32[32,32]{1,0:T(8,128)S(1)}, s32[32,32]{1,0:T(8,128)}, u32[]{:S(2)}) copy-start(s32[32,32]{1,0:T(8,128)} %param.12) | copy-start | bytes 12292
  0.6 28.7 %copy-start.17 = (bf16[176,512]{1,0:T(8,128)(2,1)S(1)}, bf16[176,512]{1,0:T(8,128)(2,1)}, u32[]{:S(2)}) copy-start(bf16[176,512]{1,0:T(8,128)(2,1)} %param.13) | copy-start | bytes 540676
  0.7 28.7 %copy-start.18 = (bf16[512,176]{0,1:T(8,128)(2,1)S(1)}, bf16[512,176]{0,1:T(8,128)(2,1)}, u32[]{:S(2)}) copy-start(bf16[512,176]{0,1:T(8,128)(2,1)} %param.15) | copy-start | bytes 540676
  3.0 9.7 %collective-permute-start.5 = (f32[45,512]{1,0:T(8,128)S(1)}, f32[45,512]{1,0:T(8,128)S(1)}, u32[]{:S(2)}, u32[]{:S(2)}) collective-permute-start(f32[45,512]{1,0:T(8,128)S(1)} %pad_maximum_fusion.1), channel_id=1, source_target_pairs={{0,4},{4,8},{8,12},{12,16},{16,20},{20,24},{24,28},{28,32},{32,36}... | collective-permute-start | bytes 276488 | tf_op jit(solution)/shard_map/ppermute | solution.py:380
  12.7 0.6 copy-start.19
  27.0 23.6 %collective-permute-start.6 = (bf16[16,48,128]{2,1,0:T(8,128)(2,1)}, bf16[16,48,128]{2,1,0:T(8,128)(2,1)S(1)}, u32[]{:S(2)}, u32[]{:S(2)}) collective-permute-start(bf16[16,48,128]{2,1,0:T(8,128)(2,1)} %get-tuple-element.26), channel_id=1, source_target_pairs={{0,16},{1,17},{2,18},{3,19},{4,20},{5,21},{6,22},{7,23},{8,24},{9,... | collective-permute-start | bytes 589832 | tf_op jit(solution)/shard_map/ppermute | solution.py:392
  27.1 9.0 %collective-permute-start = (f32[45,512]{1,0:T(8,128)S(1)}, f32[45,512]{1,0:T(8,128)S(1)}, u32[]{:S(2)}, u32[]{:S(2)}) collective-permute-start(f32[45,512]{1,0:T(8,128)S(1)} %pad_maximum_fusion), channel_id=1, source_target_pairs={{0,124},{4,0},{8,4},{12,8},{16,12},{20,16},{24,20},{28,24},{32,28}... | collective-permute-start | bytes 276488 | tf_op jit(solution)/shard_map/ppermute | solution.py:381
  31.0 22.2 %collective-permute-start.7 = (bf16[16,48,128]{2,1,0:T(8,128)(2,1)}, bf16[16,48,128]{2,1,0:T(8,128)(2,1)S(1)}, u32[]{:S(2)}, u32[]{:S(2)}) collective-permute-start(bf16[16,48,128]{2,1,0:T(8,128)(2,1)} %get-tuple-element.27), channel_id=1, source_target_pairs={{0,17},{1,16},{2,19},{3,18},{4,21},{5,20},{6,23},{7,22},{8,25},{9,... | collective-permute-start | bytes 589832 | tf_op jit(solution)/shard_map/ppermute | solution.py:392
  31.8 24.1 %collective-permute-start.8 = (bf16[16,48,128]{2,1,0:T(8,128)(2,1)}, bf16[16,48,128]{2,1,0:T(8,128)(2,1)S(1)}, u32[]{:S(2)}, u32[]{:S(2)}) collective-permute-start(bf16[16,48,128]{2,1,0:T(8,128)(2,1)} %get-tuple-element.28), channel_id=1, source_target_pairs={{0,18},{1,19},{2,16},{3,17},{4,22},{5,23},{6,20},{7,21},{8,26},{9,... | collective-permute-start | bytes 589832 | tf_op jit(solution)/shard_map/ppermute | solution.py:392
  36.0 19.9 %collective-permute-start.9 = (bf16[16,48,128]{2,1,0:T(8,128)(2,1)}, bf16[16,48,128]{2,1,0:T(8,128)(2,1)S(1)}, u32[]{:S(2)}, u32[]{:S(2)}) collective-permute-start(bf16[16,48,128]{2,1,0:T(8,128)(2,1)} %get-tuple-element.29), channel_id=1, source_target_pairs={{0,19},{1,18},{2,17},{3,16},{4,23},{5,22},{6,21},{7,20},{8,27},{9,... | collective-permute-start | bytes 589832 | tf_op jit(solution)/shard_map/ppermute | solution.py:392
  36.0 0.6 copy-start.20
  50.4 16.9 %collective-permute-start.1 = (bf16[16,48,128]{2,1,0:T(8,128)(2,1)}, bf16[16,48,128]{2,1,0:T(8,128)(2,1)S(1)}, u32[]{:S(2)}, u32[]{:S(2)}) collective-permute-start(bf16[16,48,128]{2,1,0:T(8,128)(2,1)} %get-tuple-element.22), channel_id=1, source_target_pairs={{0,16},{1,17},{2,18},{3,19},{4,20},{5,21},{6,22},{7,23},{8,24},{9,... | collective-permute-start | bytes 589832 | tf_op jit(solution)/shard_map/ppermute | solution.py:392
  50.5 6.1 %copy-start.9 = (bf16[16,48,128]{2,1,0:T(8,128)(2,1)}, bf16[16,48,128]{2,1,0:T(8,128)(2,1)S(1)}, u32[]{:S(2)}) copy-start(bf16[16,48,128]{2,1,0:T(8,128)(2,1)S(1)} %collective-permute-done.6.m0) | copy-start | bytes 589828
  50.6 18.9 %collective-permute-start.2 = (bf16[16,48,128]{2,1,0:T(8,128)(2,1)}, bf16[16,48,128]{2,1,0:T(8,128)(2,1)S(1)}, u32[]{:S(2)}, u32[]{:S(2)}) collective-permute-start(bf16[16,48,128]{2,1,0:T(8,128)(2,1)} %get-tuple-element.23), channel_id=1, source_target_pairs={{0,17},{1,16},{2,19},{3,18},{4,21},{5,20},{6,23},{7,22},{8,25},{9,... | collective-permute-start | bytes 589832 | tf_op jit(solution)/shard_map/ppermute | solution.py:392
  53.2 3.4 %copy-start.13 = (bf16[16,48,128]{2,1,0:T(8,128)(2,1)}, bf16[16,48,128]{2,1,0:T(8,128)(2,1)S(1)}, u32[]{:S(2)}) copy-start(bf16[16,48,128]{2,1,0:T(8,128)(2,1)S(1)} %collective-permute-done.7.m1) | copy-start | bytes 589828
  53.2 18.8 %collective-permute-start.3 = (bf16[16,48,128]{2,1,0:T(8,128)(2,1)}, bf16[16,48,128]{2,1,0:T(8,128)(2,1)S(1)}, u32[]{:S(2)}, u32[]{:S(2)}) collective-permute-start(bf16[16,48,128]{2,1,0:T(8,128)(2,1)} %get-tuple-element.24), channel_id=1, source_target_pairs={{0,18},{1,19},{2,16},{3,17},{4,22},{5,23},{6,20},{7,21},{8,26},{9,... | collective-permute-start | bytes 589832 | tf_op jit(solution)/shard_map/ppermute | solution.py:392
  55.9 0.7 copy-start.15
  55.9 16.1 %collective-permute-start.4 = (bf16[16,48,128]{2,1,0:T(8,128)(2,1)}, bf16[16,48,128]{2,1,0:T(8,128)(2,1)S(1)}, u32[]{:S(2)}, u32[]{:S(2)}) collective-permute-start(bf16[16,48,128]{2,1,0:T(8,128)(2,1)} %get-tuple-element.25), channel_id=1, source_target_pairs={{0,19},{1,18},{2,17},{3,16},{4,23},{5,22},{6,21},{7,20},{8,27},{9,... | collective-permute-start | bytes 589832 | tf_op jit(solution)/shard_map/ppermute | solution.py:392
  55.9 0.7 copy-start.16
  67.3 16.1 %collective-permute-start.14 = (bf16[16,48,128]{2,1,0:T(8,128)(2,1)}, bf16[16,48,128]{2,1,0:T(8,128)(2,1)S(1)}, u32[]{:S(2)}, u32[]{:S(2)}) collective-permute-start(bf16[16,48,128]{2,1,0:T(8,128)(2,1)} %get-tuple-element.36), channel_id=1, source_target_pairs={{0,16},{1,17},{2,18},{3,19},{4,20},{5,21},{6,22},{7,23},{8,24},{9,... | collective-permute-start | bytes 589832 | tf_op jit(solution)/shard_map/ppermute | solution.py:398
  67.4 4.7 %copy-start.10 = (bf16[16,48,128]{2,1,0:T(8,128)(2,1)}, bf16[16,48,128]{2,1,0:T(8,128)(2,1)S(1)}, u32[]{:S(2)}) copy-start(bf16[16,48,128]{2,1,0:T(8,128)(2,1)S(1)} %collective-permute-done.1.m0) | copy-start | bytes 589828
  67.4 18.2 %collective-permute-start.15 = (bf16[16,48,128]{2,1,0:T(8,128)(2,1)}, bf16[16,48,128]{2,1,0:T(8,128)(2,1)S(1)}, u32[]{:S(2)}, u32[]{:S(2)}) collective-permute-start(bf16[16,48,128]{2,1,0:T(8,128)(2,1)} %get-tuple-element.37), channel_id=1, source_target_pairs={{0,17},{1,16},{2,19},{3,18},{4,21},{5,20},{6,23},{7,22},{8,25},{9,... | collective-permute-start | bytes 589832 | tf_op jit(solution)/shard_map/ppermute | solution.py:398
  69.4 2.6 %copy-start.11 = (bf16[16,48,128]{2,1,0:T(8,128)(2,1)}, bf16[16,48,128]{2,1,0:T(8,128)(2,1)S(1)}, u32[]{:S(2)}) copy-start(bf16[16,48,128]{2,1,0:T(8,128)(2,1)S(1)} %collective-permute-done.2.m1) | copy-start | bytes 589828
  69.4 18.7 %collective-permute-start.16 = (bf16[16,48,128]{2,1,0:T(8,128)(2,1)}, bf16[16,48,128]{2,1,0:T(8,128)(2,1)S(1)}, u32[]{:S(2)}, u32[]{:S(2)}) collective-permute-start(bf16[16,48,128]{2,1,0:T(8,128)(2,1)} %get-tuple-element.38), channel_id=1, source_target_pairs={{0,18},{1,19},{2,16},{3,17},{4,22},{5,23},{6,20},{7,21},{8,26},{9,... | collective-permute-start | bytes 589832 | tf_op jit(solution)/shard_map/ppermute | solution.py:398
  72.0 0.7 copy-start.12
  72.0 28.3 %collective-permute-start.17 = (bf16[16,48,128]{2,1,0:T(8,128)(2,1)}, bf16[16,48,128]{2,1,0:T(8,128)(2,1)S(1)}, u32[]{:S(2)}, u32[]{:S(2)}) collective-permute-start(bf16[16,48,128]{2,1,0:T(8,128)(2,1)} %get-tuple-element.39), channel_id=1, source_target_pairs={{0,19},{1,18},{2,17},{3,16},{4,23},{5,22},{6,21},{7,20},{8,27},{9,... | collective-permute-start | bytes 589832 | tf_op jit(solution)/shard_map/ppermute | solution.py:398
  72.1 0.7 copy-start.14
  83.4 23.3 %collective-permute-start.10 = (bf16[16,48,128]{2,1,0:T(8,128)(2,1)}, bf16[16,48,128]{2,1,0:T(8,128)(2,1)S(1)}, u32[]{:S(2)}, u32[]{:S(2)}) collective-permute-start(bf16[16,48,128]{2,1,0:T(8,128)(2,1)} %get-tuple-element.31), channel_id=1, source_target_pairs={{0,16},{1,17},{2,18},{3,19},{4,20},{5,21},{6,22},{7,23},{8,24},{9,... | collective-permute-start | bytes 589832 | tf_op jit(solution)/shard_map/ppermute | solution.py:398
  83.5 16.8 %copy-start.1 = (bf16[16,48,128]{2,1,0:T(8,128)(2,1)}, bf16[16,48,128]{2,1,0:T(8,128)(2,1)S(1)}, u32[]{:S(2)}) copy-start(bf16[16,48,128]{2,1,0:T(8,128)(2,1)S(1)} %collective-permute-done.14.refs_1_) | copy-start | bytes 589828
  83.5 23.3 %collective-permute-start.11 = (bf16[16,48,128]{2,1,0:T(8,128)(2,1)}, bf16[16,48,128]{2,1,0:T(8,128)(2,1)S(1)}, u32[]{:S(2)}, u32[]{:S(2)}) collective-permute-start(bf16[16,48,128]{2,1,0:T(8,128)(2,1)} %get-tuple-element.32), channel_id=1, source_target_pairs={{0,17},{1,16},{2,19},{3,18},{4,21},{5,20},{6,23},{7,22},{8,25},{9,... | collective-permute-start | bytes 589832 | tf_op jit(solution)/shard_map/ppermute | solution.py:398
  85.5 14.8 %copy-start.2 = (bf16[16,48,128]{2,1,0:T(8,128)(2,1)}, bf16[16,48,128]{2,1,0:T(8,128)(2,1)S(1)}, u32[]{:S(2)}) copy-start(bf16[16,48,128]{2,1,0:T(8,128)(2,1)S(1)} %collective-permute-done.15.refs_2_) | copy-start | bytes 589828
  85.5 21.2 %collective-permute-start.12 = (bf16[16,48,128]{2,1,0:T(8,128)(2,1)}, bf16[16,48,128]{2,1,0:T(8,128)(2,1)S(1)}, u32[]{:S(2)}, u32[]{:S(2)}) collective-permute-start(bf16[16,48,128]{2,1,0:T(8,128)(2,1)} %get-tuple-element.33), channel_id=1, source_target_pairs={{0,18},{1,19},{2,16},{3,17},{4,22},{5,23},{6,20},{7,21},{8,26},{9,... | collective-permute-start | bytes 589832 | tf_op jit(solution)/shard_map/ppermute | solution.py:398
  88.1 12.2 %copy-start.3 = (bf16[16,48,128]{2,1,0:T(8,128)(2,1)}, bf16[16,48,128]{2,1,0:T(8,128)(2,1)S(1)}, u32[]{:S(2)}) copy-start(bf16[16,48,128]{2,1,0:T(8,128)(2,1)S(1)} %collective-permute-done.16.refs_3_) | copy-start | bytes 589828
  88.1 18.7 %collective-permute-start.13 = (bf16[16,48,128]{2,1,0:T(8,128)(2,1)}, bf16[16,48,128]{2,1,0:T(8,128)(2,1)S(1)}, u32[]{:S(2)}, u32[]{:S(2)}) collective-permute-start(bf16[16,48,128]{2,1,0:T(8,128)(2,1)} %get-tuple-element.34), channel_id=1, source_target_pairs={{0,19},{1,18},{2,17},{3,16},{4,23},{5,22},{6,21},{7,20},{8,27},{9,... | collective-permute-start | bytes 589832 | tf_op jit(solution)/shard_map/ppermute | solution.py:398
  100.3 0.7 copy-start.4
  106.7 0.7 copy-start.5
  106.7 0.7 copy-start.6
  106.8 0.8 copy-start.7
  106.8 0.8 copy-start.8
where the time goes:
time: 114 us; the launch traced here: 113 us
  Pallas kernels  60.2 us (53%)
  starting transfers between devices  23.6 us (21%)
  blocking collectives  11.5 us (10%)
  local copies, waits for them, and re-layouts  10.7 us (9%)
  waiting for transfers between devices  4.33 us (4%)
  other arithmetic  1.97 us (2%)
    pallas_call x2, Pallas kernels, advect_call(): pl.pallas_call(body, out_shape=out_shape, in_specs=in_specs, out_specs=[h...  27.4 us
    pallas_call x2, Pallas kernels, network_call(): pl.pallas_call(network_body, out_shape=[shape] * 4 + [jax.ShapeDtypeStruc...  21.4 us
    all_to_all x1, blocking collectives, local(): lax.all_to_all(heat, 'panel', split_axis=0, concat_axis=0, tiled=True)  11.5 us
    pallas_call x2, Pallas kernels, apply_call(): pl.pallas_call(body, out_shape=jax.ShapeDtypeStruct((1, L, BY, NX), f32),...  11.5 us
    ppermute x8, starting transfers between devices, local(): arrived[k] = [lax.ppermute(m, AXES, cross(i)) for i, m in enumerate(msgs)]  9.92 us
    ppermute x8, starting transfers between devices, local(): returned[k] = [lax.ppermute(t, AXES, cross(i)) for i, t in enumerate(tends)]  9.37 us
    ppermute x1, waiting for transfers between devices, local(): above = lax.ppermute(last, 'panel', ring(1))  4.28 us
    unnamed x44, local copies, waits for them, and re-layouts  3.55 us
  transfers between devices with their start and end apart: 18, of which 1 were waited for; matrix products, arithmetic and copies ran while one was open for 6% of the time, Pallas kernels for 36%

commit v1 on v0

v1 whole, which is shorter than its diff:
```python
import jax
import jax.numpy as jnp
from jax import lax
from jax.experimental import pallas as pl
from jax.experimental.pallas import tpu as pltpu
from jax.sharding import PartitionSpec as P


F = 4
L = 44
LP = 48
BY = 128
NX = 512
HID = 512
NB = 32
K = 2
ORDER = (0, 1)
R = BY // K
NBK = R // 4
RC = R // 2
SB = 8
CH = 4
ROOM = 59 << 20
NET_ROOM = 32 << 20
LV = 4
U = 4
LC = 11
NC = L // LC
NG = L // LV
AXES = ("panel", "span")
f32 = jnp.float32
bf16 = jnp.bfloat16


def position():
    return lax.axis_index("panel"), lax.axis_index("span")


def coarse_row(b):
    return 8 * (b // 4) + 4 * (b % 2) + (b % 4) // 2


def lane_iota(shape):
    return lax.broadcasted_iota(jnp.int32, shape, len(shape) - 1)


def row_iota(shape):
    return lax.broadcasted_iota(jnp.int32, shape, len(shape) - 2)


def shift_right(tiles):
    n = len(tiles)
    rolled = [pltpu.roll(t, 1, 1) for t in tiles]
    first = lane_iota(tiles[0].shape) == 0
    return [jnp.where(first, rolled[(t - 1) % n], rolled[t]) for t in range(n)]


def shift_left(tiles):
    n = len(tiles)
    rolled = [pltpu.roll(t, 127, 1) for t in tiles]
    last = lane_iota(tiles[0].shape) == 127
    return [jnp.where(last, rolled[(t + 1) % n], rolled[t]) for t in range(n)]


def advect_body(k, *refs):
    top = k == 0
    bottom = k == K - 1
    refs = list(refs)
    flips = refs.pop(0)
    scale = refs.pop(0)
    state = refs.pop(0)
    wind = refs.pop(0)
    halo = refs.pop(0) if top or bottom else None
    moved = refs.pop(0)
    msgs = [refs.pop(0) for _ in range(4)]
    cells, out, coef, pairs, pool, in_sem, out_sem = refs[:7]
    edge = refs[7] if top or bottom else None
    here, span = position()
    off = 0 if top else 8
    r0 = k * R
    first = r0 - off
    count = R + 16 - (8 if top else 0) - (8 if bottom else 0)

    def fetch(g, t):
        return pltpu.make_async_copy(
            state.at[pl.ds(g * LV, LV), first : first + count, 128 * t : 128 * (t + 1)],
            cells.at[t, pl.ds(g * LV, LV)],
            in_sem.at[g, t],
        )

    def store(g):
        return pltpu.make_async_copy(
            out.at[pl.ds(g * LV, LV)], moved.at[pl.ds(g * LV, LV)], out_sem.at[g]
        )

    for g in range(NG):
        for t in range(4):
            fetch(g, t).start()
    if edge is not None:
        flag = flips[here] if top else flips[(here + 1) % NB]
        anti = (row_iota((128, 128)) + lane_iota((128, 128)) == 127).astype(f32)
        for t in range(4):
            turned = jnp.dot(
                halo[:, 128 * (3 - t) : 128 * (4 - t)],
                anti,
                precision=lax.Precision.HIGHEST,
                preferred_element_type=f32,
            )
            edge[t, 0 : L + 1] = jnp.where(flag == 1, turned, halo[:, 128 * t : 128 * (t + 1)])
    cols = [slice(128 * t, 128 * (t + 1)) for t in range(4)]
    u = [wind[0, r0 : r0 + R, c] for c in cols]
    v = [wind[1, r0 : r0 + R, c] for c in cols]
    rows = row_iota((R, 128))
    if top:
        above = [
            jnp.where(rows == 0, edge[t, L : L + 1], pltpu.roll(w, 1, 0)) for t, w in enumerate(v)
        ]
    else:
        above = [wind[1, r0 - 1 : r0 + R - 1, c] for c in cols]
    if bottom:
        below = [
            jnp.where(rows == R - 1, edge[t, L : L + 1], pltpu.roll(w, R - 1, 0))
            for t, w in enumerate(v)
        ]
    else:
        below = [wind[1, r0 + 1 : r0 + R + 1, c] for c in cols]
    left = shift_right(u)
    face = [0.5 * (a + b) for a, b in zip(left, u)]
    plus = [jnp.maximum(w, 0.0) for w in face]
    minus = [jnp.minimum(w, 0.0) for w in face]
    next_plus = shift_left(plus)
    next_minus = shift_left(minus)
    for t in range(4):
        lower = 0.5 * (above[t] + v[t])
        upper = 0.5 * (v[t] + below[t])
        lower_plus = jnp.maximum(lower, 0.0)
        lower_minus = jnp.minimum(lower, 0.0)
        upper_plus = jnp.maximum(upper, 0.0)
        upper_minus = jnp.minimum(upper, 0.0)
        coef[5 * t] = next_plus[t] - minus[t] + upper_plus - lower_minus
        coef[5 * t + 1] = next_minus[t]
        coef[5 * t + 2] = -plus[t]
        coef[5 * t + 3] = upper_minus
        coef[5 * t + 4] = -lower_plus
    quarter = jnp.where(row_iota((256, 128)) // 2 == lane_iota((256, 128)), 0.25, 0.0).astype(bf16)

    even = row_iota((8, 128)) % 2 == 0
    rows8 = row_iota((8, 128))

    def cell_rows(l, s, start):
        at = off + start
        band = slice(start, start + 8)
        q = [cells[t, l, at : at + 8, :] for t in range(4)]
        west = shift_right(q)
        east = shift_left(q)
        new = []
        for t in range(4):
            if top and start == 0:
                up = jnp.where(rows8 == 0, edge[t, pl.ds(l, 1), :], pltpu.roll(q[t], 1, 0))
            else:
                up = cells[t, l, at - 1 : at + 7, :]
            if bottom and start == R - 8:
                down = jnp.where(rows8 == 7, edge[t, pl.ds(l, 1), :], pltpu.roll(q[t], 7, 0))
            else:
                down = cells[t, l, at + 1 : at + 9, :]
            change = (
                coef[5 * t, band] * q[t]
                + coef[5 * t + 1, band] * east[t]
                + coef[5 * t + 2, band] * west[t]
                + coef[5 * t + 3, band] * down
                + coef[5 * t + 4, band] * up
            )
            new.append(q[t] - s * change)
            out[l, band, 128 * t : 128 * (t + 1)] = new[t]
        return new

    def group(g, carry):
        for t in range(4):
            fetch(g, t).wait()

        def levels(m, carry):
            for n in range(R // 16):
                for w in range(U):
                    l = g * LV + m * U + w
                    s = scale[l]
                    upper = cell_rows(l, s, 16 * n)
                    lower = cell_rows(l, s, 16 * n + 8)
                    at = pl.multiple_of(l * RC + 8 * n, 8)
                    for t in range(4):
                        pairs[t, pl.ds(at, 8), :] = jnp.where(
                            even,
                            upper[t] + pltpu.roll(upper[t], 7, 0),
                            lower[t] + pltpu.roll(lower[t], 1, 0),
                        )
            return carry

        lax.fori_loop(0, LV // U, levels, 0)
        store(g).start()
        return carry

    lax.fori_loop(0, NG, group, 0)

    def pool_rows(g, carry):
        start = pl.multiple_of(g * (LC * RC), 8)
        for half in range(2):
            block = jnp.concatenate(
                [pairs[2 * half, pl.ds(start, LC * RC)], pairs[2 * half + 1, pl.ds(start, LC * RC)]], axis=1
            )
            high = block.astype(bf16)
            low = (block - high.astype(f32)).astype(bf16)
            pooled = jnp.dot(high, quarter, preferred_element_type=f32)
            pooled += jnp.dot(low, quarter, preferred_element_type=f32)
            pool[pl.ds(pl.multiple_of(half * LP * RC + start, 8), LC * RC), :] = pooled
        return carry

    lax.fori_loop(0, NC, pool_rows, 0)
    valid = row_iota((LP, 128)) < L
    for i in range(4):
        c = span ^ i
        base = (c & 1) * (LP * RC) + (c >> 1) * 2
        for b in range(NBK):
            column = pool[pl.ds(base + coarse_row(b), LP, stride=RC), :]
            msgs[i][b] = jnp.where(valid, column, 0.0).astype(bf16)
    for g in range(NG):
        store(g).wait()


def advect_call(k, flips, scale, state, wind, halo):
    top = k == 0
    bottom = k == K - 1
    count = R + 16 - (8 if top else 0) - (8 if bottom else 0)
    smem = pl.BlockSpec(memory_space=pltpu.SMEM)
    vmem = pl.BlockSpec(memory_space=pltpu.VMEM)
    hbm = pl.BlockSpec(memory_space=pltpu.HBM)
    in_specs = [smem, smem, hbm, vmem]
    operands = [flips, scale, state, wind]
    scratch = [
        pltpu.VMEM((4, L, count, 128), f32),
        pltpu.VMEM((L, R, NX), f32),
        pltpu.VMEM((20, R, 128), f32),
        pltpu.VMEM((4, L * RC, 128), f32),
        pltpu.VMEM((2 * LP * RC, 128), f32),
        pltpu.SemaphoreType.DMA((NG, 4)),
        pltpu.SemaphoreType.DMA((NG,)),
    ]
    if top or bottom:
        in_specs.append(vmem)
        operands.append(halo)
        scratch.append(pltpu.VMEM((4, LP, 128), f32))
    out_shape = [jax.ShapeDtypeStruct((L, R, NX), f32)]
    out_shape += [jax.ShapeDtypeStruct((NBK, LP, 128), bf16)] * 4

    def body(*refs):
        advect_body(k, *refs)

    return pl.pallas_call(
        body,
        out_shape=out_shape,
        in_specs=in_specs,
        out_specs=[hbm] + [vmem] * 4,
        compiler_params=pltpu.CompilerParams(vmem_limit_bytes=ROOM),
        scratch_shapes=scratch,
    )(*operands)


def silu(z):
    half = 0.5 * z
    return half + half * jnp.tanh(half)


def network_body(k, dest, m0, m1, m2, m3, w_in, w_mid, w_out, heat_in, o0, o1, o2, o3, heat, xs, ts, wi, wo):
    here, c = position()
    served = here ^ 4
    heat[...] = heat_in[...]
    ins = (m0, m1, m2, m3)
    outs = (o0, o1, o2, o3)
    none = jnp.zeros((LP - L, HID), bf16)
    for f in range(F):
        rows = slice(LP * f, LP * (f + 1))
        wi[rows] = jnp.concatenate([w_in[L * f : L * (f + 1)], none], axis=0)
        wo[rows] = jnp.concatenate([w_out[L * f : L * (f + 1)], none], axis=0)
    for i in range(4):
        at = pl.multiple_of((c ^ i) * LP, LP)
        for b in range(NBK):
            xs[b // SB, pl.ds(at, LP), 128 * (b % SB) : 128 * (b % SB + 1)] = ins[i][b]

    def part(j, carry):
        wide = xs[j].astype(f32)
        inv = lax.rsqrt(jnp.sum(wide * wide, axis=0, keepdims=True) * (1.0 / (F * L)) + 1e-05)
        normed = (wide * inv).T.astype(bf16)
        size = SB * 128 // CH
        hid = []
        for n in range(CH):
            z = jnp.dot(normed[n * size : (n + 1) * size], wi[...], preferred_element_type=f32)
            hid.append(silu(z).astype(bf16))
        for layer in range(4):
            for n in range(CH):
                z = jnp.dot(hid[n], w_mid[layer], preferred_element_type=f32)
                hid[n] = (hid[n].astype(f32) + silu(z)).astype(bf16)
        parts = [
            lax.dot_general(wo[...], h, (((1,), (1,)), ((), ())), preferred_element_type=f32)
            for h in hid
        ]
        for n in range(CH):
            ts[j, :, n * size : (n + 1) * size] = parts[n].astype(bf16)
            warm = jnp.sum(parts[n][0:L], axis=0, keepdims=True) * (L**-0.5)
            for b in range(SB // CH):
                row = dest[served, k * NBK + j * SB + n * (SB // CH) + b]
                heat[pl.ds(row, 1), :] = warm[:, 128 * b : 128 * (b + 1)]
        return carry

    lax.fori_loop(0, NBK // SB, part, 0)
    for i in range(4):
        at = pl.multiple_of((c ^ i) * LP, LP)
        for b in range(NBK):
            outs[i][b] = ts[b // SB, pl.ds(at, LP), 128 * (b % SB) : 128 * (b % SB + 1)]


def network_call(k, dest, msgs, w_in, w_mid, w_out, heat):
    smem = pl.BlockSpec(memory_space=pltpu.SMEM)
    vmem = pl.BlockSpec(memory_space=pltpu.VMEM)
    shape = jax.ShapeDtypeStruct((NBK, LP, 128), bf16)

    def body(*refs):
        network_body(k, *refs)

    return pl.pallas_call(
        body,
        out_shape=[shape] * 4 + [jax.ShapeDtypeStruct((NB, 128), f32)],
        in_specs=[smem] + [vmem] * 8,
        out_specs=[vmem] * 5,
        compiler_params=pltpu.CompilerParams(vmem_limit_bytes=NET_ROOM),
        scratch_shapes=[
            pltpu.VMEM((NBK // SB, F * LP, SB * 128), bf16),
            pltpu.VMEM((NBK // SB, F * LP, SB * 128), bf16),
            pltpu.VMEM((F * LP, HID), bf16),
            pltpu.VMEM((F * LP, HID), bf16),
        ],
    )(dest, *msgs, w_in, w_mid, w_out, heat)


def apply_body(k, first, *refs):
    refs = list(refs)
    ins = [refs.pop(0) for _ in range(4)]
    moved = refs.pop(0)
    other = refs.pop(0)
    final = refs.pop(0)
    if first:
        refs.pop(0)[...] = other[...]
    cells, spread, in_sem, out_sem = refs
    _, span = position()

    def fetch(g):
        return pltpu.make_async_copy(
            moved.at[pl.ds(g * LC, LC)], cells.at[pl.ds(g * LC, LC)], in_sem.at[g]
        )

    def store(g):
        return pltpu.make_async_copy(
            cells.at[pl.ds(g * LC, LC)],
            final.at[0, pl.ds(g * LC, LC), k * R : (k + 1) * R, :],
            out_sem.at[g],
        )

    for g in range(NC):
        fetch(g).start()
    for i in range(4):
        c = span ^ i
        base = (c & 1) * (LP * R) + (c >> 1) * 2
        for b in range(NBK):
            spread[pl.ds(base + 4 * b, LP, stride=R), :] = ins[i][b].astype(f32)
    twice = (row_iota((128, 256)) == lane_iota((128, 256)) // 2).astype(bf16)
    even = row_iota((LC * R, 128)) % 2 == 0

    def group(g, carry):
        fetch(g).wait()
        for half in range(2):
            start = pl.multiple_of(half * LP * R + g * (LC * R), 8)
            coarse = spread[pl.ds(start, LC * R), :]
            coarse = jnp.where(even, coarse, pltpu.roll(coarse, 1, 0)).astype(bf16)
            fine = jnp.dot(coarse, twice, preferred_element_type=f32)
            lanes = slice(256 * half, 256 * (half + 1))
            at = pl.ds(g * LC, LC)
            cells[at, :, lanes] = cells[at, :, lanes] + fine.reshape(LC, R, 256)
        store(g).start()
        return carry

    lax.fori_loop(0, NC, group, 0)
    for g in range(NC):
        store(g).wait()


def apply_call(k, tends, moved, buffer, heat):
    vmem = pl.BlockSpec(memory_space=pltpu.VMEM)
    hbm = pl.BlockSpec(memory_space=pltpu.HBM)
    first = buffer is None
    in_specs = [vmem] * 4 + [hbm, vmem if first else hbm]
    operands = [*tends, moved, heat if first else buffer]
    out_shape = [jax.ShapeDtypeStruct((1, L, BY, NX), f32)]
    out_specs = [hbm]
    if first:
        out_shape.append(jax.ShapeDtypeStruct((NB, 128), f32))
        out_specs.append(vmem)

    def body(*refs):
        apply_body(k, first, *refs)

    return pl.pallas_call(
        body,
        out_shape=out_shape,
        in_specs=in_specs,
        out_specs=out_specs,
        scratch_shapes=[
            pltpu.VMEM((L, R, NX), f32),
            pltpu.VMEM((2 * LP * R, 128), f32),
            pltpu.SemaphoreType.DMA((NC,)),
            pltpu.SemaphoreType.DMA((NC,)),
        ],
        compiler_params=pltpu.CompilerParams(vmem_limit_bytes=ROOM),
        input_output_aliases={} if first else {5: 0},
    )(*operands)


def edges_body(state, wind, first, last, rows, winds, sem):
    copies = []
    for n, row in enumerate((0, BY - 1)):
        copies.append(pltpu.make_async_copy(state.at[:, row, :], rows.at[n], sem.at[n, 0]))
        copies.append(pltpu.make_async_copy(wind.at[1, row : row + 1, :], winds.at[n], sem.at[n, 1]))
    for copy in copies:
        copy.start()
    for copy in copies:
        copy.wait()
    for n, result in enumerate((first, last)):
        result[0:L] = rows[n]
        result[L : L + 1] = winds[n]


def edges_call(state, wind):
    hbm = pl.BlockSpec(memory_space=pltpu.HBM)
    vmem = pl.BlockSpec(memory_space=pltpu.VMEM)
    return pl.pallas_call(
        edges_body,
        out_shape=[jax.ShapeDtypeStruct((L + 1, NX), f32)] * 2,
        in_specs=[hbm, hbm],
        out_specs=[vmem, vmem],
        scratch_shapes=[
            pltpu.VMEM((2, L, NX), f32),
            pltpu.VMEM((2, 1, NX), f32),
            pltpu.SemaphoreType.DMA((2, 2)),
        ],
        compiler_params=pltpu.CompilerParams(vmem_limit_bytes=ROOM),
        name="edges",
    )(state, wind)


def ring(step):
    return [(i, (i + step) % NB) for i in range(NB)]


def cross(i):
    return [(p * F + s, (p ^ 4) * F + (s ^ i)) for p in range(NB) for s in range(F)]


def local(state, wind, level_scale, edge_flip, block_dest, weight_in, weight_mid, weight_out):
    field = state[0]
    first, last = edges_call(field, wind)
    above = lax.ppermute(last, "panel", ring(1))
    below = lax.ppermute(first, "panel", ring(-1))
    moved = {}
    arrived = {}
    for k in ORDER:
        halo = above if k == 0 else below
        moved[k], *msgs = advect_call(k, edge_flip, level_scale, field, wind, halo)
        arrived[k] = [lax.ppermute(m, AXES, cross(i)) for i, m in enumerate(msgs)]
    heat = jnp.zeros((NB, 128), f32)
    returned = {}
    for k in ORDER:
        *tends, heat = network_call(k, block_dest, arrived[k], weight_in, weight_mid, weight_out.T, heat)
        returned[k] = [lax.ppermute(t, AXES, cross(i)) for i, t in enumerate(tends)]
    new_state = None
    for k in ORDER:
        new_state, *passed = apply_call(k, returned[k], moved[k], new_state, heat)
        if passed:
            slots = lax.all_to_all(passed[0], "panel", split_axis=0, concat_axis=0, tiled=True)
    heating = slots.reshape(4, 2, 4, 128)[:, ::-1].reshape(NB * 128)
    return (new_state, heating)


def solution(mesh):
    placed = (P("span", None, "panel", None), P(None, "panel", None), P(), P(), P(), P(), P(), P())
    return jax.shard_map(
        local,
        mesh=mesh,
        in_specs=placed,
        out_specs=(P("span", None, "panel", None), P(("panel", "span"))),
        check_vma=False,
    )
```

time: 114 us -> 95.9 us (0.84)
  blocking collectives: 11.5 us -> 0 us
  Pallas kernels: 60.2 us -> 52.3 us
  local copies, waits for them, and re-layouts: 10.7 us -> 4.05 us
  starting transfers between devices: 23.6 us -> 29.5 us
  waiting for transfers between devices: 4.33 us -> 8.36 us
  other arithmetic: 1.97 us -> 0 us
    all_to_all x1 -> x0, blocking collectives: 11.5 us -> none  [local(): lax.all_to_all(heat, 'panel', split_axis=0, concat_axis=0, tiled=True)]
    pallas_call x2, Pallas kernels: 27.4 us -> 21.1 us  [advect_call(): pl.pallas_call(body, out_shape=out_shape, in_specs=in_specs, out_specs=[h...]
    all_to_all x0 -> x1, starting transfers between devices: none -> 6.18 us  [local(): lax.all_to_all(passed[0], 'panel', split_axis=0, concat_axis=0, tiled=True)]
    ppermute x1, waiting for transfers between devices: 4.28 us -> 7.78 us  [local(): above = lax.ppermute(last, 'panel', ring(1))]
    slice x2 -> x0, local copies, waits for them, and re-layouts: 2.15 us -> none  [the longest x1 1.49 us: local(): state[0, :, BY - 1, :]]
    another operation x1 -> x0, other arithmetic: 1.94 us -> none  [local(): jnp.stack([span, edge_flip[here], edge_flip[(here + 1) % NB]])]
    pallas_call x4 -> x5, Pallas kernels: 32.8 us -> 31.1 us  [the longest x2 17.4 us: network_call(): pl.pallas_call(body, out_shape=[shape] * 4 + [jax.ShapeDtypeStruct((NB, 1...]
    dynamic_slice x2 -> x0, local copies, waits for them, and re-layouts: 1.33 us -> none  [the longest x1 1.33 us: local(): edge_flip[here]]
  transfers between devices with their start and end apart: 18 -> 19, of which waited for: 1 -> 2; matrix products, arithmetic and copies ran while one was open for 6% -> 0% of each run, Pallas kernels for 36% -> 42%
where the time goes in v1:
time: 95.9 us; the launch traced here: 95.1 us
  Pallas kernels  52.3 us (55%)
  starting transfers between devices  29.5 us (31%)
  waiting for transfers between devices  8.36 us (9%)
  local copies, waits for them, and re-layouts  4.05 us (4%)
    pallas_call x2, Pallas kernels, advect_call(): pl.pallas_call(body, out_shape=out_shape, in_specs=in_specs, out_specs=[h...  21.1 us
    pallas_call x2, Pallas kernels, network_call(): pl.pallas_call(body, out_shape=[shape] * 4 + [jax.ShapeDtypeStruct((NB, 1...  17.4 us
    pallas_call x2, Pallas kernels, apply_call(): pl.pallas_call(body, out_shape=out_shape, in_specs=in_specs, out_specs=ou...  12 us
    ppermute x8, starting transfers between devices, local(): arrived[k] = [lax.ppermute(m, AXES, cross(i)) for i, m in enumerate(msgs)]  10.8 us
    ppermute x8, starting transfers between devices, local(): returned[k] = [lax.ppermute(t, AXES, cross(i)) for i, t in enumerate(tends)]  9.47 us
    ppermute x1, waiting for transfers between devices, local(): above = lax.ppermute(last, 'panel', ring(1))  7.78 us
    all_to_all x1, starting transfers between devices, local(): lax.all_to_all(passed[0], 'panel', split_axis=0, concat_axis=0, tiled=True)  6.18 us
    unnamed x32, local copies, waits for them, and re-layouts  3.44 us
  transfers between devices with their start and end apart: 19, of which 2 were waited for; matrix products, arithmetic and copies ran while one was open for 0% of the time, Pallas kernels for 42%

profile of v1, /device:TPU:1, one launch (start us, length us, event | category | flops | bytes accessed | tf_op | source)
XLA Modules:
  0.0 95.1 jit_solution(10040364678670134298)
XLA Ops:
  0.6 1.7 %edges.1 = (f32[45,512]{1,0:T(8,128)}, f32[45,512]{1,0:T(8,128)}) custom-call(f32[44,128,512]{2,1,0:T(8,128)} %bitcast.9, f32[2,128,512]{2,1,0:T(8,128)} %refs_3_.3), custom_call_target="tpu_custom_call" | custom-call | tf_op jit(solution)/shard_map/edges/pallas_call | solution.py:441
  2.3 0.0 copy-start.15
  2.3 0.0 copy-start
  2.4 0.0 copy-start.1
  2.4 0.0 copy-start.2
  2.4 0.0 copy-start.3
  2.4 2.1 %collective-permute-start.5 = (f32[45,512]{1,0:T(8,128)}, f32[45,512]{1,0:T(8,128)S(1)}, u32[]{:S(2)}, u32[]{:S(2)}) collective-permute-start(f32[45,512]{1,0:T(8,128)} %get-tuple-element.31), channel_id=1, source_target_pairs={{0,4},{4,8},{8,12},{12,16},{16,20},{20,24},{24,28},{28,32},{32,36}... | collective-permute-start | bytes 276488 | tf_op jit(solution)/shard_map/ppermute | solution.py:467
  4.5 7.8 %collective-permute-done.5.refs_4_ = f32[45,512]{1,0:T(8,128)S(1)} collective-permute-done((f32[45,512]{1,0:T(8,128)}, f32[45,512]{1,0:T(8,128)S(1)}, u32[]{:S(2)}, u32[]{:S(2)}) %collective-permute-start.5) | collective-permute-done | bytes 92192 | tf_op jit(solution)/shard_map/ppermute | solution.py:467
  12.3 0.6 copy-done.14
  12.9 10.6 %shard_map.96 = (f32[44,64,512]{2,1,0:T(8,128)}, bf16[16,48,128]{2,1,0:T(8,128)(2,1)}, bf16[16,48,128]{2,1,0:T(8,128)(2,1)}, bf16[16,48,128]{2,1,0:T(8,128)(2,1)}, bf16[16,48,128]{2,1,0:T(8,128)(2,1)}) custom-call(s32[32]{0:T(128)} %refs_0_.5, f32[44]{0:T(128)} %refs_1_.3, f32[44,128,512]{2,1,0:T(8,128)} %bitcast.10, f32[2,128,512]{2,1,0:T(8,128)} %refs_3_.3, ...), custom_call_target="tpu_custom_call" | custom-call | tf_op jit(solution)/shard_map/pallas_call | solution.py:256
  23.5 0.1 collective-permute-start.6
  23.6 0.0 copy-done.15
  23.6 1.0 %collective-permute-start = (f32[45,512]{1,0:T(8,128)S(1)}, f32[45,512]{1,0:T(8,128)S(1)}, u32[]{:S(2)}, u32[]{:S(2)}) collective-permute-start(f32[45,512]{1,0:T(8,128)S(1)} %copy-done.15), channel_id=1, source_target_pairs={{0,124},{4,0},{8,4},{12,8},{16,12},{20,16},{24,20},{28,24},{32,28}... | collective-permute-start | bytes 276488 | tf_op jit(solution)/shard_map/ppermute | solution.py:468
  24.6 1.8 %collective-permute-start.7 = (bf16[16,48,128]{2,1,0:T(8,128)(2,1)}, bf16[16,48,128]{2,1,0:T(8,128)(2,1)S(1)}, u32[]{:S(2)}, u32[]{:S(2)}) collective-permute-start(bf16[16,48,128]{2,1,0:T(8,128)(2,1)} %get-tuple-element.33), channel_id=1, source_target_pairs={{0,17},{1,16},{2,19},{3,18},{4,21},{5,20},{6,23},{7,22},{8,25},{9,... | collective-permute-start | bytes 589832 | tf_op jit(solution)/shard_map/ppermute | solution.py:474
  26.5 4.1 %collective-permute-start.8 = (bf16[16,48,128]{2,1,0:T(8,128)(2,1)}, bf16[16,48,128]{2,1,0:T(8,128)(2,1)S(1)}, u32[]{:S(2)}, u32[]{:S(2)}) collective-permute-start(bf16[16,48,128]{2,1,0:T(8,128)(2,1)} %get-tuple-element.34), channel_id=1, source_target_pairs={{0,18},{1,19},{2,16},{3,17},{4,22},{5,23},{6,20},{7,21},{8,26},{9,... | collective-permute-start | bytes 589832 | tf_op jit(solution)/shard_map/ppermute | solution.py:474
  30.5 0.0 collective-permute-start.9
  30.5 0.0 collective-permute-done.refs_4_
  30.5 0.6 copy-done.13
  31.2 10.5 %shard_map.95 = (f32[44,64,512]{2,1,0:T(8,128)}, bf16[16,48,128]{2,1,0:T(8,128)(2,1)}, bf16[16,48,128]{2,1,0:T(8,128)(2,1)}, bf16[16,48,128]{2,1,0:T(8,128)(2,1)}, bf16[16,48,128]{2,1,0:T(8,128)(2,1)}) custom-call(s32[32]{0:T(128)} %refs_0_.5, f32[44]{0:T(128)} %refs_1_.3, f32[44,128,512]{2,1,0:T(8,128)} %bitcast.11, f32[2,128,512]{2,1,0:T(8,128)} %refs_3_.3, ...), custom_call_target="tpu_custom_call" | custom-call | tf_op jit(solution)/shard_map/pallas_call | solution.py:256
  41.7 0.1 collective-permute-start.1
  41.8 0.0 collective-permute-done.6.refs_1_
  41.8 2.0 %collective-permute-start.2 = (bf16[16,48,128]{2,1,0:T(8,128)(2,1)}, bf16[16,48,128]{2,1,0:T(8,128)(2,1)S(1)}, u32[]{:S(2)}, u32[]{:S(2)}) collective-permute-start(bf16[16,48,128]{2,1,0:T(8,128)(2,1)} %get-tuple-element.28), channel_id=1, source_target_pairs={{0,17},{1,16},{2,19},{3,18},{4,21},{5,20},{6,23},{7,22},{8,25},{9,... | collective-permute-start | bytes 589832 | tf_op jit(solution)/shard_map/ppermute | solution.py:474
  43.8 0.0 collective-permute-done.7.refs_2_
  43.8 2.7 %collective-permute-start.3 = (bf16[16,48,128]{2,1,0:T(8,128)(2,1)}, bf16[16,48,128]{2,1,0:T(8,128)(2,1)S(1)}, u32[]{:S(2)}, u32[]{:S(2)}) collective-permute-start(bf16[16,48,128]{2,1,0:T(8,128)(2,1)} %get-tuple-element.29), channel_id=1, source_target_pairs={{0,18},{1,19},{2,16},{3,17},{4,22},{5,23},{6,20},{7,21},{8,26},{9,... | collective-permute-start | bytes 589832 | tf_op jit(solution)/shard_map/ppermute | solution.py:474
  46.5 0.0 collective-permute-done.8.refs_3_
  46.5 0.0 collective-permute-start.4
  46.5 0.0 collective-permute-done.9.refs_4_
  46.5 0.0 copy-done
  46.5 8.7 %shard_map.97 = (bf16[16,48,128]{2,1,0:T(8,128)(2,1)S(1)}, bf16[16,48,128]{2,1,0:T(8,128)(2,1)S(1)}, bf16[16,48,128]{2,1,0:T(8,128)(2,1)S(1)}, bf16[16,48,128]{2,1,0:T(8,128)(2,1)S(1)}, f32[32,128]{1,0:T(8,128)S(1)}) custom-call(s32[32,32]{1,0:T(8,128)S(1)} %copy-done.3, bf16[16,48,128]{2,1,0:T(8,128)(2,1)S(1)} %collective-permute-done.6.refs_1_, ...), custom_call_target="tpu_custom_call" | custom-call | tf_op jit(solution)/shard_map/pallas_call | solution.py:327
  55.3 0.1 collective-permute-start.14
  55.4 0.0 collective-permute-done.1.refs_1_
  55.4 2.1 %collective-permute-start.15 = (bf16[16,48,128]{2,1,0:T(8,128)(2,1)S(1)}, bf16[16,48,128]{2,1,0:T(8,128)(2,1)S(1)}, u32[]{:S(2)}, u32[]{:S(2)}) collective-permute-start(bf16[16,48,128]{2,1,0:T(8,128)(2,1)S(1)} %get-tuple-element.43), channel_id=1, source_target_pairs={{0,17},{1,16},{2,19},{3,18},{4,21},{5,20},{6,23},{7,22},{8,25},{9,... | collective-permute-start | bytes 589832 | tf_op jit(solution)/shard_map/ppermute | solution.py:479
  57.4 0.0 collective-permute-done.2.refs_2_
  57.4 2.6 %collective-permute-start.16 = (bf16[16,48,128]{2,1,0:T(8,128)(2,1)S(1)}, bf16[16,48,128]{2,1,0:T(8,128)(2,1)S(1)}, u32[]{:S(2)}, u32[]{:S(2)}) collective-permute-start(bf16[16,48,128]{2,1,0:T(8,128)(2,1)S(1)} %get-tuple-element.44), channel_id=1, source_target_pairs={{0,18},{1,19},{2,16},{3,17},{4,22},{5,23},{6,20},{7,21},{8,26},{9,... | collective-permute-start | bytes 589832 | tf_op jit(solution)/shard_map/ppermute | solution.py:479
  60.0 0.0 collective-permute-done.3.refs_3_
  60.0 0.0 collective-permute-start.17
  60.1 0.0 collective-permute-done.4.refs_4_
  60.1 8.7 %shard_map.98 = (bf16[16,48,128]{2,1,0:T(8,128)(2,1)S(1)}, bf16[16,48,128]{2,1,0:T(8,128)(2,1)S(1)}, bf16[16,48,128]{2,1,0:T(8,128)(2,1)S(1)}, bf16[16,48,128]{2,1,0:T(8,128)(2,1)S(1)}, f32[32,128]{1,0:T(8,128)S(1)}) custom-call(s32[32,32]{1,0:T(8,128)S(1)} %copy-done.3, bf16[16,48,128]{2,1,0:T(8,128)(2,1)S(1)} %collective-permute-done.1.refs_1_, ...), custom_call_target="tpu_custom_call" | custom-call | tf_op jit(solution)/shard_map/pallas_call | solution.py:327
  68.8 0.0 copy-start.4
  68.8 0.6 copy-done.4
  69.4 0.0 collective-permute-start.10
  69.4 0.0 collective-permute-done.14.refs_0_
  69.4 2.1 %collective-permute-start.11 = (bf16[16,48,128]{2,1,0:T(8,128)(2,1)S(1)}, bf16[16,48,128]{2,1,0:T(8,128)(2,1)S(1)}, u32[]{:S(2)}, u32[]{:S(2)}) collective-permute-start(bf16[16,48,128]{2,1,0:T(8,128)(2,1)S(1)} %get-tuple-element.38), channel_id=1, source_target_pairs={{0,17},{1,16},{2,19},{3,18},{4,21},{5,20},{6,23},{7,22},{8,25},{9,... | collective-permute-start | bytes 589832 | tf_op jit(solution)/shard_map/ppermute | solution.py:479
  71.5 0.0 collective-permute-done.15.refs_1_
  71.5 2.6 %collective-permute-start.12 = (bf16[16,48,128]{2,1,0:T(8,128)(2,1)S(1)}, bf16[16,48,128]{2,1,0:T(8,128)(2,1)S(1)}, u32[]{:S(2)}, u32[]{:S(2)}) collective-permute-start(bf16[16,48,128]{2,1,0:T(8,128)(2,1)S(1)} %get-tuple-element.39), channel_id=1, source_target_pairs={{0,18},{1,19},{2,16},{3,17},{4,22},{5,23},{6,20},{7,21},{8,26},{9,... | collective-permute-start | bytes 589832 | tf_op jit(solution)/shard_map/ppermute | solution.py:479
  74.1 0.0 collective-permute-done.16.refs_2_
  74.1 0.0 collective-permute-start.13
  74.1 0.0 collective-permute-done.17.refs_3_
  74.1 0.6 copy-done.11
  74.8 0.1 copy-done.12
  74.9 6.3 %shard_map.99 = (f32[1,44,128,512]{3,2,1,0:T(8,128)}, f32[32,128]{1,0:T(8,128)}) custom-call(bf16[16,48,128]{2,1,0:T(8,128)(2,1)} %copy-done.9, bf16[16,48,128]{2,1,0:T(8,128)(2,1)} %copy-done.10, bf16[16,48,128]{2,1,0:T(8,128)(2,1)} %copy-done.11, bf16[16,48,128]{2,1,0:T(8,128)(2,1)} %copy-done.12, f32[44,64,512]{2,1,0:T(8,128)} %get-tuple-element.46.refs_4_, ...), custom_call_target="tpu_custom_call" | custom-call | tf_op jit(solution)/shard_map/pallas_call | solution.py:408
  81.2 6.2 %all-to-all-start = ((f32[32,1,128]{2,1,0:T(1,128)}), f32[32,1,128]{2,1,0:T(1,128)S(1)}, u32[]{:S(2)}, u32[]{:S(2)}) async-start(f32[32,1,128]{2,1,0:T(1,128)} %bitcast.13), calls=%async_computation | async-start | bytes 32768 | tf_op jit(solution)/shard_map/all_to_all | solution.py:484
  87.4 0.0 collective-permute-done.10.refs_0_
  87.4 0.0 collective-permute-done.11.refs_1_
  87.4 0.0 copy-start.6
  87.4 0.0 collective-permute-done.12.refs_2_
  87.4 0.0 collective-permute-done.13.refs_3_
  87.4 0.6 copy-done.5
  88.0 0.1 copy-done.6
  88.1 0.1 copy-done.7
  88.2 0.1 copy-done.8
  88.3 5.7 %shard_map.100 = f32[1,44,128,512]{3,2,1,0:T(8,128)} custom-call(bf16[16,48,128]{2,1,0:T(8,128)(2,1)} %copy-done.5, bf16[16,48,128]{2,1,0:T(8,128)(2,1)} %copy-done.6, bf16[16,48,128]{2,1,0:T(8,128)(2,1)} %copy-done.7, bf16[16,48,128]{2,1,0:T(8,128)(2,1)} %copy-done.8, f32[44,64,512]{2,1,0:T(8,128)} %get-tuple-element.41.refs_4_, ...), custom_call_target="tpu_custom_call", output_to_operand_aliasing={{}: (5, {})} | custom-call | tf_op jit(solution)/shard_map/pallas_call | solution.py:408
  94.0 0.5 all-to-all-done
  94.5 0.6 rev.3
  (15 shorter events, 0.0 us)
Async XLA Ops:
  2.3 21.3 %copy-start.15 = (f32[45,512]{1,0:T(8,128)S(1)}, f32[45,512]{1,0:T(8,128)}, u32[]{:S(2)}) copy-start(f32[45,512]{1,0:T(8,128)} %get-tuple-element.26) | copy-start | bytes 276484
  2.3 44.2 %copy-start = (bf16[4,512,512]{2,1,0:T(8,128)(2,1)S(1)}, bf16[4,512,512]{2,1,0:T(8,128)(2,1)}, u32[]{:S(2)}) copy-start(bf16[4,512,512]{2,1,0:T(8,128)(2,1)} %refs_6_.3) | copy-start | bytes 6291460
  2.4 44.2 %copy-start.1 = (bf16[176,512]{1,0:T(8,128)(2,1)S(1)}, bf16[176,512]{1,0:T(8,128)(2,1)}, u32[]{:S(2)}) copy-start(bf16[176,512]{1,0:T(8,128)(2,1)} %refs_5_.3) | copy-start | bytes 540676
  2.4 44.2 %copy-start.2 = (bf16[512,176]{0,1:T(8,128)(2,1)S(1)}, bf16[512,176]{0,1:T(8,128)(2,1)}, u32[]{:S(2)}) copy-start(bf16[512,176]{0,1:T(8,128)(2,1)} %param.15) | copy-start | bytes 540676
  2.4 44.2 %copy-start.3 = (s32[32,32]{1,0:T(8,128)S(1)}, s32[32,32]{1,0:T(8,128)}, u32[]{:S(2)}) copy-start(s32[32,32]{1,0:T(8,128)} %refs_0_.7) | copy-start | bytes 12292
  2.4 9.9 %collective-permute-start.5 = (f32[45,512]{1,0:T(8,128)}, f32[45,512]{1,0:T(8,128)S(1)}, u32[]{:S(2)}, u32[]{:S(2)}) collective-permute-start(f32[45,512]{1,0:T(8,128)} %get-tuple-element.31), channel_id=1, source_target_pairs={{0,4},{4,8},{8,12},{12,16},{16,20},{20,24},{24,28},{28,32},{32,36}... | collective-permute-start | bytes 276488 | tf_op jit(solution)/shard_map/ppermute | solution.py:467
  12.3 0.6 copy-start.14
  23.5 18.3 %collective-permute-start.6 = (bf16[16,48,128]{2,1,0:T(8,128)(2,1)}, bf16[16,48,128]{2,1,0:T(8,128)(2,1)S(1)}, u32[]{:S(2)}, u32[]{:S(2)}) collective-permute-start(bf16[16,48,128]{2,1,0:T(8,128)(2,1)} %get-tuple-element.32), channel_id=1, source_target_pairs={{0,16},{1,17},{2,18},{3,19},{4,20},{5,21},{6,22},{7,23},{8,24},{9,... | collective-permute-start | bytes 589832 | tf_op jit(solution)/shard_map/ppermute | solution.py:474
  23.6 6.9 %collective-permute-start = (f32[45,512]{1,0:T(8,128)S(1)}, f32[45,512]{1,0:T(8,128)S(1)}, u32[]{:S(2)}, u32[]{:S(2)}) collective-permute-start(f32[45,512]{1,0:T(8,128)S(1)} %copy-done.15), channel_id=1, source_target_pairs={{0,124},{4,0},{8,4},{12,8},{16,12},{20,16},{24,20},{28,24},{32,28}... | collective-permute-start | bytes 276488 | tf_op jit(solution)/shard_map/ppermute | solution.py:468
  24.6 19.2 %collective-permute-start.7 = (bf16[16,48,128]{2,1,0:T(8,128)(2,1)}, bf16[16,48,128]{2,1,0:T(8,128)(2,1)S(1)}, u32[]{:S(2)}, u32[]{:S(2)}) collective-permute-start(bf16[16,48,128]{2,1,0:T(8,128)(2,1)} %get-tuple-element.33), channel_id=1, source_target_pairs={{0,17},{1,16},{2,19},{3,18},{4,21},{5,20},{6,23},{7,22},{8,25},{9,... | collective-permute-start | bytes 589832 | tf_op jit(solution)/shard_map/ppermute | solution.py:474
  26.5 20.0 %collective-permute-start.8 = (bf16[16,48,128]{2,1,0:T(8,128)(2,1)}, bf16[16,48,128]{2,1,0:T(8,128)(2,1)S(1)}, u32[]{:S(2)}, u32[]{:S(2)}) collective-permute-start(bf16[16,48,128]{2,1,0:T(8,128)(2,1)} %get-tuple-element.34), channel_id=1, source_target_pairs={{0,18},{1,19},{2,16},{3,17},{4,22},{5,23},{6,20},{7,21},{8,26},{9,... | collective-permute-start | bytes 589832 | tf_op jit(solution)/shard_map/ppermute | solution.py:474
  30.5 16.0 %collective-permute-start.9 = (bf16[16,48,128]{2,1,0:T(8,128)(2,1)}, bf16[16,48,128]{2,1,0:T(8,128)(2,1)S(1)}, u32[]{:S(2)}, u32[]{:S(2)}) collective-permute-start(bf16[16,48,128]{2,1,0:T(8,128)(2,1)} %get-tuple-element.35), channel_id=1, source_target_pairs={{0,19},{1,18},{2,17},{3,16},{4,23},{5,22},{6,21},{7,20},{8,27},{9,... | collective-permute-start | bytes 589832 | tf_op jit(solution)/shard_map/ppermute | solution.py:474
  30.5 0.6 copy-start.13
  41.7 13.7 %collective-permute-start.1 = (bf16[16,48,128]{2,1,0:T(8,128)(2,1)}, bf16[16,48,128]{2,1,0:T(8,128)(2,1)S(1)}, u32[]{:S(2)}, u32[]{:S(2)}) collective-permute-start(bf16[16,48,128]{2,1,0:T(8,128)(2,1)} %get-tuple-element.27), channel_id=1, source_target_pairs={{0,16},{1,17},{2,18},{3,19},{4,20},{5,21},{6,22},{7,23},{8,24},{9,... | collective-permute-start | bytes 589832 | tf_op jit(solution)/shard_map/ppermute | solution.py:474
  41.8 15.7 %collective-permute-start.2 = (bf16[16,48,128]{2,1,0:T(8,128)(2,1)}, bf16[16,48,128]{2,1,0:T(8,128)(2,1)S(1)}, u32[]{:S(2)}, u32[]{:S(2)}) collective-permute-start(bf16[16,48,128]{2,1,0:T(8,128)(2,1)} %get-tuple-element.28), channel_id=1, source_target_pairs={{0,17},{1,16},{2,19},{3,18},{4,21},{5,20},{6,23},{7,22},{8,25},{9,... | collective-permute-start | bytes 589832 | tf_op jit(solution)/shard_map/ppermute | solution.py:474
  43.8 16.2 %collective-permute-start.3 = (bf16[16,48,128]{2,1,0:T(8,128)(2,1)}, bf16[16,48,128]{2,1,0:T(8,128)(2,1)S(1)}, u32[]{:S(2)}, u32[]{:S(2)}) collective-permute-start(bf16[16,48,128]{2,1,0:T(8,128)(2,1)} %get-tuple-element.29), channel_id=1, source_target_pairs={{0,18},{1,19},{2,16},{3,17},{4,22},{5,23},{6,20},{7,21},{8,26},{9,... | collective-permute-start | bytes 589832 | tf_op jit(solution)/shard_map/ppermute | solution.py:474
  46.5 13.6 %collective-permute-start.4 = (bf16[16,48,128]{2,1,0:T(8,128)(2,1)}, bf16[16,48,128]{2,1,0:T(8,128)(2,1)S(1)}, u32[]{:S(2)}, u32[]{:S(2)}) collective-permute-start(bf16[16,48,128]{2,1,0:T(8,128)(2,1)} %get-tuple-element.30), channel_id=1, source_target_pairs={{0,19},{1,18},{2,17},{3,16},{4,23},{5,22},{6,21},{7,20},{8,27},{9,... | collective-permute-start | bytes 589832 | tf_op jit(solution)/shard_map/ppermute | solution.py:474
  55.3 14.1 %collective-permute-start.14 = (bf16[16,48,128]{2,1,0:T(8,128)(2,1)S(1)}, bf16[16,48,128]{2,1,0:T(8,128)(2,1)S(1)}, u32[]{:S(2)}, u32[]{:S(2)}) collective-permute-start(bf16[16,48,128]{2,1,0:T(8,128)(2,1)S(1)} %get-tuple-element.42), channel_id=1, source_target_pairs={{0,16},{1,17},{2,18},{3,19},{4,20},{5,21},{6,22},{7,23},{8,24},{9,... | collective-permute-start | bytes 589832 | tf_op jit(solution)/shard_map/ppermute | solution.py:479
  55.4 16.1 %collective-permute-start.15 = (bf16[16,48,128]{2,1,0:T(8,128)(2,1)S(1)}, bf16[16,48,128]{2,1,0:T(8,128)(2,1)S(1)}, u32[]{:S(2)}, u32[]{:S(2)}) collective-permute-start(bf16[16,48,128]{2,1,0:T(8,128)(2,1)S(1)} %get-tuple-element.43), channel_id=1, source_target_pairs={{0,17},{1,16},{2,19},{3,18},{4,21},{5,20},{6,23},{7,22},{8,25},{9,... | collective-permute-start | bytes 589832 | tf_op jit(solution)/shard_map/ppermute | solution.py:479
  57.4 16.6 %collective-permute-start.16 = (bf16[16,48,128]{2,1,0:T(8,128)(2,1)S(1)}, bf16[16,48,128]{2,1,0:T(8,128)(2,1)S(1)}, u32[]{:S(2)}, u32[]{:S(2)}) collective-permute-start(bf16[16,48,128]{2,1,0:T(8,128)(2,1)S(1)} %get-tuple-element.44), channel_id=1, source_target_pairs={{0,18},{1,19},{2,16},{3,17},{4,22},{5,23},{6,20},{7,21},{8,26},{9,... | collective-permute-start | bytes 589832 | tf_op jit(solution)/shard_map/ppermute | solution.py:479
  60.0 14.1 %collective-permute-start.17 = (bf16[16,48,128]{2,1,0:T(8,128)(2,1)S(1)}, bf16[16,48,128]{2,1,0:T(8,128)(2,1)S(1)}, u32[]{:S(2)}, u32[]{:S(2)}) collective-permute-start(bf16[16,48,128]{2,1,0:T(8,128)(2,1)S(1)} %get-tuple-element.45), channel_id=1, source_target_pairs={{0,19},{1,18},{2,17},{3,16},{4,23},{5,22},{6,21},{7,20},{8,27},{9,... | collective-permute-start | bytes 589832 | tf_op jit(solution)/shard_map/ppermute | solution.py:479
  68.8 0.6 copy-start.4
  69.4 18.0 %collective-permute-start.10 = (bf16[16,48,128]{2,1,0:T(8,128)(2,1)S(1)}, bf16[16,48,128]{2,1,0:T(8,128)(2,1)S(1)}, u32[]{:S(2)}, u32[]{:S(2)}) collective-permute-start(bf16[16,48,128]{2,1,0:T(8,128)(2,1)S(1)} %get-tuple-element.37), channel_id=1, source_target_pairs={{0,16},{1,17},{2,18},{3,19},{4,20},{5,21},{6,22},{7,23},{8,24},{9,... | collective-permute-start | bytes 589832 | tf_op jit(solution)/shard_map/ppermute | solution.py:479
  69.4 4.7 %copy-start.9 = (bf16[16,48,128]{2,1,0:T(8,128)(2,1)}, bf16[16,48,128]{2,1,0:T(8,128)(2,1)S(1)}, u32[]{:S(2)}) copy-start(bf16[16,48,128]{2,1,0:T(8,128)(2,1)S(1)} %collective-permute-done.14.refs_0_) | copy-start | bytes 589828
  69.4 18.0 %collective-permute-start.11 = (bf16[16,48,128]{2,1,0:T(8,128)(2,1)S(1)}, bf16[16,48,128]{2,1,0:T(8,128)(2,1)S(1)}, u32[]{:S(2)}, u32[]{:S(2)}) collective-permute-start(bf16[16,48,128]{2,1,0:T(8,128)(2,1)S(1)} %get-tuple-element.38), channel_id=1, source_target_pairs={{0,17},{1,16},{2,19},{3,18},{4,21},{5,20},{6,23},{7,22},{8,25},{9,... | collective-permute-start | bytes 589832 | tf_op jit(solution)/shard_map/ppermute | solution.py:479
  71.5 2.6 %copy-start.10 = (bf16[16,48,128]{2,1,0:T(8,128)(2,1)}, bf16[16,48,128]{2,1,0:T(8,128)(2,1)S(1)}, u32[]{:S(2)}) copy-start(bf16[16,48,128]{2,1,0:T(8,128)(2,1)S(1)} %collective-permute-done.15.refs_1_) | copy-start | bytes 589828
  71.5 15.9 %collective-permute-start.12 = (bf16[16,48,128]{2,1,0:T(8,128)(2,1)S(1)}, bf16[16,48,128]{2,1,0:T(8,128)(2,1)S(1)}, u32[]{:S(2)}, u32[]{:S(2)}) collective-permute-start(bf16[16,48,128]{2,1,0:T(8,128)(2,1)S(1)} %get-tuple-element.39), channel_id=1, source_target_pairs={{0,18},{1,19},{2,16},{3,17},{4,22},{5,23},{6,20},{7,21},{8,26},{9,... | collective-permute-start | bytes 589832 | tf_op jit(solution)/shard_map/ppermute | solution.py:479
  74.1 0.7 copy-start.11
  74.1 13.3 %collective-permute-start.13 = (bf16[16,48,128]{2,1,0:T(8,128)(2,1)S(1)}, bf16[16,48,128]{2,1,0:T(8,128)(2,1)S(1)}, u32[]{:S(2)}, u32[]{:S(2)}) collective-permute-start(bf16[16,48,128]{2,1,0:T(8,128)(2,1)S(1)} %get-tuple-element.40), channel_id=1, source_target_pairs={{0,19},{1,18},{2,17},{3,16},{4,23},{5,22},{6,21},{7,20},{8,27},{9,... | collective-permute-start | bytes 589832 | tf_op jit(solution)/shard_map/ppermute | solution.py:479
  74.1 0.7 copy-start.12
  81.2 13.4 %all-to-all-start = ((f32[32,1,128]{2,1,0:T(1,128)}), f32[32,1,128]{2,1,0:T(1,128)S(1)}, u32[]{:S(2)}, u32[]{:S(2)}) async-start(f32[32,1,128]{2,1,0:T(1,128)} %bitcast.13), calls=%async_computation | async-start | bytes 32768 | tf_op jit(solution)/shard_map/all_to_all | solution.py:484
  87.4 0.7 copy-start.5
  87.4 0.7 copy-start.6
  87.4 0.8 copy-start.7
  87.4 0.8 copy-start.8
